TPU v7x, 32 devices: a whole 2x2x4 slice. The times are simulated.
32 devices in a mesh: dp: 8 (over z, x), head: 4 (over y, core).
Axes of the slice: x: 2, y: 2, z: 4, core: 2. Of those that a mesh axis runs over, the one named last changes fastest.
Arguments:
- block_input: bfloat16 [16384, 768], P(('dp', 'head')), may hold values from -6 to 6
- norm1_gain: float32 [768], replicated, may hold values from 0.5 to 1.5
- norm1_bias: float32 [768], replicated, may hold values from -0.625 to 0.625
- qkv_weight: bfloat16 [3, 768, 768], P(None, None, 'head'), may hold values from -0.21875 to 0.21875
- qkv_bias: float32 [2, 12, 64], P(None, 'head'), may hold values from -0.625 to 0.625
- proj_weight: bfloat16 [768, 768], P('head'), may hold values from -1.75 to 1.75
- proj_bias: float32 [768], replicated, may hold values from -0.625 to 0.625
- norm2_gain: float32 [768], replicated, may hold values from 0.5 to 1.5
- norm2_bias: float32 [768], replicated, may hold values from -0.625 to 0.625
- router_weight: float32 [768, 8], replicated, may hold values from -0.15625 to 0.15625
- up_weight: bfloat16 [8, 768, 3072], P('dp'), may hold values from -0.21875 to 0.21875
- up_bias: float32 [8, 3072], P('dp'), may hold values from -0.625 to 0.625
- down_weight: bfloat16 [8, 3072, 768], P('dp'), may hold values from -1.25 to 1.25
- down_bias: float32 [8, 768], P('dp'), may hold values from -5 to 5
- routes: int32 [16384, 1], P(('dp', 'head')), may hold values from 0 to 7; in each aligned block of 512 rows (0 to 511, 512 to 1023, ...) at most 128 rows name the same one
- lengths: int32 [8, 4], P('dp'), may hold values from 1 to 1024, 2048 in all within a row
- cotangent: bfloat16 [16384, 768], P(('dp', 'head')), may hold values from -6 to 6
Outputs:
- mixed: bfloat16 [16384, 768], P(('dp', 'head'))
- balance: float32 [32], P(('dp', 'head'))
- input_grad: float32 [16384, 768], P(('dp', 'head'))
- norm1_gain_grad: float32 [768], P(('dp', 'head'))
- norm1_bias_grad: float32 [768], P(('dp', 'head'))
- qkv_weight_grad: float32 [3, 768, 768], P(None, 'dp', 'head')
- qkv_bias_grad: float32 [2, 12, 64], P(None, 'head', 'dp')
- proj_weight_grad: float32 [768, 768], P('head', 'dp')
- proj_bias_grad: float32 [768], P(('dp', 'head'))
- norm2_gain_grad: float32 [768], P(('dp', 'head'))
- norm2_bias_grad: float32 [768], P(('dp', 'head'))
- router_weight_grad: float32 [768, 8], P(('dp', 'head'))
- up_weight_grad: float32 [8, 768, 3072], P('dp', None, 'head')
- up_bias_grad: float32 [8, 3072], P('dp', 'head')
- down_weight_grad: float32 [8, 3072, 768], P('dp', 'head')
- down_bias_grad: float32 [8, 768], P('dp', 'head')
Inputs may be any that keep to these rules, and one draw needn't show every extreme that they name: `routes`: among the rows of one device at most 128 name the same expert. `lengths`: each row sums to 2048, and its largest entry is 1024.
All inputs are finite; a program needn't handle non-finite values.
Results may differ from a plain program's by a relative error of at most 0.017.
Values may be sent and summed in bfloat16 or wider, within the bound.
A program may use at most 192 MiB of HBM per device.

v0:
```python
import jax
import jax.numpy as jnp
from jax import lax
from jax.sharding import PartitionSpec as P

EPSILON = 1e-05
BAL_COEF = 0.01
HIGHEST = lax.Precision.HIGHEST
NEG_LARGE = -1e30


def normalize(values, gain, bias):
    average = jnp.mean(values, axis=-1, keepdims=True)
    centred = values - average
    variance = jnp.mean(centred * centred, axis=-1, keepdims=True)
    inverse = lax.rsqrt(variance + EPSILON)
    scaled = centred * inverse
    return (scaled * gain + bias, scaled, inverse)


def norm_backward(grad_normed, scaled, inverse, gain):
    grad_scaled = grad_normed * gain
    first_mean = jnp.mean(grad_scaled, axis=-1, keepdims=True)
    second_mean = jnp.mean(grad_scaled * scaled, axis=-1, keepdims=True)
    return inverse * (grad_scaled - first_mean - scaled * second_mean)


def local(
    block_input,
    norm1_gain,
    norm1_bias,
    qkv_weight,
    qkv_bias,
    proj_weight,
    proj_bias,
    norm2_gain,
    norm2_bias,
    router_weight,
    up_weight,
    up_bias,
    down_weight,
    down_bias,
    routes,
    lengths,
    cotangent,
):
    tok_rows, width = block_input.shape
    input_float = block_input.astype(jnp.float32)
    normed_one, scaled_one, inverse_one = normalize(input_float, norm1_gain, norm1_bias)
    gathered = lax.all_gather(normed_one.astype(jnp.bfloat16), "head", axis=0, tiled=True)
    group_rows = gathered.shape[0]
    local_heads = qkv_bias.shape[1]
    head_size = qkv_bias.shape[2]
    local_cols = local_heads * head_size
    head_shape = (group_rows, local_heads, head_size)
    projected = jnp.einsum("td,cde->cte", gathered, qkv_weight, preferred_element_type=jnp.float32)
    queries = (projected[0] + qkv_bias[0].reshape(-1)).astype(jnp.bfloat16).reshape(head_shape)
    keys_all = projected[1].astype(jnp.bfloat16).reshape(head_shape)
    values_all = (projected[2] + qkv_bias[1].reshape(-1)).astype(jnp.bfloat16).reshape(head_shape)
    positions = jnp.arange(group_rows, dtype=jnp.int32)
    seq_ends = jnp.cumsum(lengths[0])
    segment = jnp.sum((positions[:, None] >= seq_ends[None, :]).astype(jnp.int32), axis=1)
    block_rows = min(512, group_rows)
    blocks = group_rows // block_rows
    score_scale = head_size ** (-0.5)

    def block_scores(first_row):
        query_block = lax.dynamic_slice_in_dim(queries, first_row, block_rows, 0)
        seg_block = lax.dynamic_slice_in_dim(segment, first_row, block_rows, 0)
        pos_block = first_row + jnp.arange(block_rows, dtype=jnp.int32)
        allowed = (seg_block[:, None] == segment[None, :]) & (
            positions[None, :] <= pos_block[:, None]
        )
        scores = (
            jnp.einsum("qhd,khd->hqk", query_block, keys_all, preferred_element_type=jnp.float32)
            * score_scale
        )
        return (query_block, jnp.where(allowed[None], scores, NEG_LARGE))

    def attend_block(state_in, block_index):
        query_block, scores = block_scores(block_index * block_rows)
        row_max = jnp.max(scores, axis=-1, keepdims=True)
        exponent = jnp.exp(scores - row_max)
        row_total = jnp.sum(exponent, axis=-1, keepdims=True)
        probability = exponent / row_total
        context_block = jnp.einsum(
            "hqk,khd->qhd",
            probability.astype(jnp.bfloat16),
            values_all,
            preferred_element_type=jnp.float32,
        )
        return (
            state_in,
            (context_block.astype(jnp.bfloat16), (row_max + jnp.log(row_total))[..., 0]),
        )

    unused_state, (context_blocks, lse_blocks) = lax.scan(
        attend_block, jnp.zeros((), jnp.float32), jnp.arange(blocks)
    )
    context = context_blocks.reshape(group_rows, local_cols)
    piece = context
    attended = lax.psum_scatter(
        jnp.dot(piece, proj_weight, preferred_element_type=jnp.float32),
        "head",
        scatter_dimension=0,
        tiled=True,
    )
    residual = input_float + attended + proj_bias
    normed_two, scaled_two, inverse_two = normalize(residual, norm2_gain, norm2_bias)
    num_experts = router_weight.shape[1]
    capacity = 2 * tok_rows // num_experts
    logits = jnp.dot(
        normed_two, router_weight, precision=HIGHEST, preferred_element_type=jnp.float32
    )
    probability = jax.nn.softmax(logits, axis=-1)
    expert_id = routes[:, 0]
    one_hot = (expert_id[:, None] == jnp.arange(num_experts, dtype=jnp.int32)[None, :]).astype(
        jnp.int32
    )
    slot_index = jnp.sum(jnp.cumsum(one_hot, axis=0) * one_hot, axis=1) - 1
    flat_index = expert_id * capacity + slot_index
    hot_float = one_hot.astype(jnp.float32)
    gate_value = jnp.sum(probability * hot_float, axis=1)
    fraction = jnp.mean(hot_float, axis=0)
    balance = num_experts * jnp.sum(fraction * jnp.mean(probability, axis=0))
    send_rows = (
        jnp.zeros((num_experts * capacity, width), jnp.bfloat16)
        .at[flat_index]
        .set(normed_two.astype(jnp.bfloat16))
    )
    received = lax.all_to_all(
        send_rows.reshape(num_experts, capacity, width),
        "dp",
        split_axis=0,
        concat_axis=0,
        tiled=True,
    )
    expert_rows = received.reshape(num_experts * capacity, width)
    preact_out = jnp.dot(expert_rows, up_weight[0], preferred_element_type=jnp.float32) + up_bias[0]
    hidden = jax.nn.gelu(preact_out, approximate=False).astype(jnp.bfloat16)
    produced = (
        jnp.dot(hidden, down_weight[0], preferred_element_type=jnp.float32) + down_bias[0]
    ).astype(jnp.bfloat16)
    returned = lax.all_to_all(
        produced.reshape(num_experts, capacity, width),
        "dp",
        split_axis=0,
        concat_axis=0,
        tiled=True,
    )
    expert_out = returned.reshape(num_experts * capacity, width)[flat_index].astype(jnp.float32)
    mixed = (residual + gate_value[:, None] * expert_out).astype(jnp.bfloat16)
    grad_out = cotangent.astype(jnp.float32)
    grad_gate = jnp.sum(grad_out * expert_out, axis=1)
    grad_produced = (gate_value[:, None] * grad_out).astype(jnp.bfloat16)
    send_grads = (
        jnp.zeros((num_experts * capacity, width), jnp.bfloat16).at[flat_index].set(grad_produced)
    )
    grads_in = lax.all_to_all(
        send_grads.reshape(num_experts, capacity, width),
        "dp",
        split_axis=0,
        concat_axis=0,
        tiled=True,
    ).reshape(num_experts * capacity, width)
    preact_back, hidden_back = (preact_out, hidden)
    grad_hidden = jnp.einsum(
        "rd,fd->rf", grads_in, down_weight[0], preferred_element_type=jnp.float32
    )
    down_grad = jnp.einsum("rf,rd->fd", hidden_back, grads_in, preferred_element_type=jnp.float32)
    down_bias_grad = jnp.sum(grads_in.astype(jnp.float32), axis=0)
    unused_value, gelu_pull = jax.vjp(
        lambda inner: jax.nn.gelu(inner, approximate=False), preact_back
    )
    grad_preact = gelu_pull(grad_hidden)[0].astype(jnp.bfloat16)
    up_grad = jnp.einsum("rd,rf->df", expert_rows, grad_preact, preferred_element_type=jnp.float32)
    up_bias_grad = jnp.sum(grad_preact.astype(jnp.float32), axis=0)
    grad_rows = jnp.einsum(
        "rf,df->rd", grad_preact, up_weight[0], preferred_element_type=jnp.float32
    ).astype(jnp.bfloat16)
    grads_back = lax.all_to_all(
        grad_rows.reshape(num_experts, capacity, width),
        "dp",
        split_axis=0,
        concat_axis=0,
        tiled=True,
    )
    grad_expert_in = grads_back.reshape(num_experts * capacity, width)[flat_index].astype(
        jnp.float32
    )
    up_sum, down_sum, up_bias_sum, down_bias_sum = (
        lax.psum_scatter(
            up_grad[None].astype(jnp.bfloat16), "head", scatter_dimension=2, tiled=True
        ).astype(jnp.float32),
        lax.psum_scatter(
            down_grad[None].astype(jnp.bfloat16), "head", scatter_dimension=1, tiled=True
        ).astype(jnp.float32),
        lax.psum_scatter(
            up_bias_grad[None].astype(jnp.bfloat16), "head", scatter_dimension=1, tiled=True
        ).astype(jnp.float32),
        lax.psum_scatter(
            down_bias_grad[None].astype(jnp.bfloat16), "head", scatter_dimension=1, tiled=True
        ).astype(jnp.float32),
    )
    grad_prob = (
        hot_float * grad_gate[:, None] + BAL_COEF * num_experts * fraction[None, :] / tok_rows
    )
    grad_logits = probability * (
        grad_prob - jnp.sum(probability * grad_prob, axis=1, keepdims=True)
    )
    grad_normed_two = grad_expert_in + jnp.einsum(
        "te,de->td",
        grad_logits,
        router_weight,
        precision=HIGHEST,
        preferred_element_type=jnp.float32,
    )
    router_grad = jnp.einsum(
        "td,te->de", normed_two, grad_logits, precision=HIGHEST, preferred_element_type=jnp.float32
    )
    gain_two_grad = jnp.sum(grad_normed_two * scaled_two, axis=0)
    bias_two_grad = jnp.sum(grad_normed_two, axis=0)
    grad_residual = grad_out + norm_backward(grad_normed_two, scaled_two, inverse_two, norm2_gain)
    proj_bias_grad = jnp.sum(grad_residual, axis=0)
    grad_local = grad_residual.astype(jnp.bfloat16)
    grad_attended = lax.all_gather(grad_local, "head", axis=0, tiled=True)
    proj_grad = jnp.einsum("tc,td->cd", context, grad_attended, preferred_element_type=jnp.float32)
    grad_context = (
        jnp.einsum("td,cd->tc", grad_attended, proj_weight, preferred_element_type=jnp.float32)
        .astype(jnp.bfloat16)
        .reshape(head_shape)
    )

    def attend_back(state_in, block_index):
        grad_keys, grad_values = state_in
        first_row = block_index * block_rows
        query_block, scores = block_scores(first_row)
        lse_block = lse_blocks[block_index]
        prob_block = jnp.exp(scores - lse_block[..., None])
        grad_ctx_block = lax.dynamic_slice_in_dim(grad_context, first_row, block_rows, 0)
        grad_prob_block = jnp.einsum(
            "qhd,khd->hqk", grad_ctx_block, values_all, preferred_element_type=jnp.float32
        )
        row_delta = jnp.sum(prob_block * grad_prob_block, axis=-1, keepdims=True)
        grad_scores = (prob_block * (grad_prob_block - row_delta)).astype(jnp.bfloat16)
        grad_query = (
            jnp.einsum("hqk,khd->qhd", grad_scores, keys_all, preferred_element_type=jnp.float32)
            * score_scale
        )
        grad_keys = (
            grad_keys
            + jnp.einsum(
                "hqk,qhd->khd", grad_scores, query_block, preferred_element_type=jnp.float32
            )
            * score_scale
        )
        grad_values = grad_values + jnp.einsum(
            "hqk,qhd->khd",
            prob_block.astype(jnp.bfloat16),
            grad_ctx_block,
            preferred_element_type=jnp.float32,
        )
        return ((grad_keys, grad_values), grad_query.astype(jnp.bfloat16))

    zero_heads = jnp.zeros(head_shape, jnp.float32)
    (grad_keys_all, grad_values_all), grad_query_blocks = lax.scan(
        attend_back, (zero_heads, zero_heads), jnp.arange(blocks)
    )
    flat_shape = (group_rows, local_cols)
    grad_proj = jnp.stack(
        [
            grad_query_blocks.reshape(flat_shape),
            grad_keys_all.astype(jnp.bfloat16).reshape(flat_shape),
            grad_values_all.astype(jnp.bfloat16).reshape(flat_shape),
        ]
    )
    qkv_grad = jnp.einsum("td,cte->cde", gathered, grad_proj, preferred_element_type=jnp.float32)
    qkv_bias_grad = jnp.stack(
        [
            jnp.sum(grad_proj[0].astype(jnp.float32), axis=0),
            jnp.sum(grad_proj[2].astype(jnp.float32), axis=0),
        ]
    ).reshape(2, local_heads, head_size)
    piece = grad_proj
    grad_normed_one = lax.psum_scatter(
        jnp.einsum("cte,cde->td", piece, qkv_weight, preferred_element_type=jnp.float32).astype(
            jnp.bfloat16
        ),
        "head",
        scatter_dimension=0,
        tiled=True,
    ).astype(jnp.float32)
    gain_one_grad = jnp.sum(grad_normed_one * scaled_one, axis=0)
    bias_one_grad = jnp.sum(grad_normed_one, axis=0)
    input_grad = grad_residual + norm_backward(grad_normed_one, scaled_one, inverse_one, norm1_gain)
    qkv_sum, proj_sum, qkv_bias_sum = (
        lax.psum_scatter(
            qkv_grad.astype(jnp.bfloat16), "dp", scatter_dimension=1, tiled=True
        ).astype(jnp.float32),
        lax.psum_scatter(
            proj_grad.astype(jnp.bfloat16), "dp", scatter_dimension=1, tiled=True
        ).astype(jnp.float32),
        lax.psum_scatter(
            qkv_bias_grad.astype(jnp.bfloat16), "dp", scatter_dimension=2, tiled=True
        ).astype(jnp.float32),
    )
    gain_one_sum, bias_one_sum, proj_bias_sum, gain_two_sum, bias_two_sum, router_sum = (
        lax.psum_scatter(gain_one_grad, ("dp", "head"), scatter_dimension=0, tiled=True),
        lax.psum_scatter(bias_one_grad, ("dp", "head"), scatter_dimension=0, tiled=True),
        lax.psum_scatter(proj_bias_grad, ("dp", "head"), scatter_dimension=0, tiled=True),
        lax.psum_scatter(gain_two_grad, ("dp", "head"), scatter_dimension=0, tiled=True),
        lax.psum_scatter(bias_two_grad, ("dp", "head"), scatter_dimension=0, tiled=True),
        lax.psum_scatter(router_grad, ("dp", "head"), scatter_dimension=0, tiled=True),
    )
    return (
        mixed,
        balance.reshape(1),
        input_grad,
        gain_one_sum,
        bias_one_sum,
        qkv_sum,
        qkv_bias_sum,
        proj_sum,
        proj_bias_sum,
        gain_two_sum,
        bias_two_sum,
        router_sum,
        up_sum,
        up_bias_sum,
        down_sum,
        down_bias_sum,
    )


def solution(mesh):
    placed = (
        P(("dp", "head"), None),
        P(),
        P(),
        P(None, None, "head"),
        P(None, "head", None),
        P("head", None),
        P(),
        P(),
        P(),
        P(),
        P("dp", None, None),
        P("dp", None),
        P("dp", None, None),
        P("dp", None),
        P(("dp", "head"), None),
        P("dp", None),
        P(("dp", "head"), None),
    )
    return jax.shard_map(
        local,
        mesh=mesh,
        in_specs=placed,
        out_specs=(
            P(("dp", "head"), None),
            P(("dp", "head")),
            P(("dp", "head"), None),
            P(("dp", "head")),
            P(("dp", "head")),
            P(None, "dp", "head"),
            P(None, "head", "dp"),
            P("head", "dp"),
            P(("dp", "head")),
            P(("dp", "head")),
            P(("dp", "head")),
            P(("dp", "head"), None),
            P("dp", None, "head"),
            P("dp", "head"),
            P("dp", "head", None),
            P("dp", "head"),
        ),
        check_vma=False,
    )
```

profile of v0, /device:TPU:0, one launch (start us, length us, event | category | flops | bytes accessed | tf_op | source)
XLA Modules:
  0.0 963.5 jit_solution(16885735443561784780)
XLA Ops:
  14.9 29.7 %all-gather.3.cloned.1.call-done = bf16[2048,768]{1,0:T(8,128)(2,1)} async-done(((bf16[512,768]{1,0:T(8,128)(2,1)}), bf16[2048,768]{1,0:T(8,128)(2,1)}) %all-gather.3.cloned.1.call-update) | async-done | bytes 3145744 | tf_op jit(solution)/shard_map/all_gather | solution.py:50
  50.2 93.1 %while.28 = (s32[]{:T(128)}, bf16[4,512,3,64]{1,3,2,0:T(8,128)(2,1)}, f32[4,3,512]{2,1,0:T(4,128)}, s32[4]{0:T(128)S(1)}, s32[2048]{0:T(1024)S(1)}, /*index=5*/b...) while((s32[]{:T(128)}, ...), condition=%wide.region_7.8_spmd.clone, body=%wide.region_4.7_spmd.clone.sunk | while | flops 846298112 | bytes 43978956 | solution.py:97
  65.8 7.3 fusion.186
  89.0 7.3 fusion.186
  135.4 7.3 fusion.186
  152.7 56.3 %reduce-scatter.19.cloned.1.call-done = f32[512,768]{1,0:T(8,128)} async-done(((f32[2048,768]{1,0:T(8,128)}), f32[512,768]{1,0:T(8,128)}) %reduce-scatter.19.cloned.1.call-update) | async-done | bytes 1572880 | tf_op jit(solution)/shard_map/reduce_scatter | solution.py:102
  223.0 37.0 %all-to-all-done = bf16[8,128,768]{2,1,0:T(8,128)(2,1)} async-done(((bf16[8,128,768]{2,1,0:T(8,128)(2,1)}), bf16[8,128,768]{2,1,0:T(8,128)(2,1)}, u32[]{:S(2)}, u32[]{:S(2)}) %all-to-all-start) | async-done | bytes 1572896 | tf_op jit(solution)/shard_map/all_to_all | solution.py:131
  260.0 36.3 %multiply_convert_fusion.1 = (bf16[1024,3072]{1,0:T(8,128)(2,1)S(1)}, f32[1024,3072]{1,0:T(8,128)}, f32[1024,3072]{1,0:T(8,128)}) fusion(f32[3072]{0:T(1024)S(1)} %bitcast.220, bf16[1024,768]{1,0:T(8,128)(2,1)} %bitcast.17, bf16[1,768,3072]{2,1,0:T(8,128)(2,1)} %param.31), kind=kOutput, calls=%fused_computation.58 | convolution fusion | flops 5039456256 | bytes 37761024 | tf_op jit(solution)/shard_map/dot_general | solution.py:139
  296.5 10.8 %add_convert_fusion.1 = bf16[1024,768]{1,0:T(8,128)(2,1)} fusion(bf16[1024,3072]{1,0:T(8,128)(2,1)S(1)} %get-tuple-element.312, bf16[1,3072,768]{2,1,0:T(8,128)(2,1)} %param.33, f32[768]{0:T(1024)S(1)} %reduce.8), kind=kOutput, calls=%fused_computation.86 | convolution fusion | flops 4833411072 | bytes 12585984 | tf_op jit(solution)/shard_map/dot_general | solution.py:142
  313.9 34.3 %all-to-all-done.1 = bf16[8,128,768]{2,1,0:T(8,128)(2,1)} async-done(((bf16[8,128,768]{2,1,0:T(8,128)(2,1)}), bf16[8,128,768]{2,1,0:T(8,128)(2,1)}, u32[]{:S(2)}, u32[]{:S(2)}) %all-to-all-start.1) | async-done | bytes 1572896 | tf_op jit(solution)/shard_map/all_to_all | solution.py:144
  359.0 40.9 %all_to_all.20 = bf16[8,128,768]{2,1,0:T(8,128)(2,1)S(1)} all-to-all(bf16[8,128,768]{2,1,0:T(8,128)(2,1)} %bitcast.187), channel_id=1, replica_groups=mesh['dp'=8,'head'=4] {'dp'}, dimensions={0} | all-to-all | bytes 3145728 | tf_op jit(solution)/shard_map/all_to_all | solution.py:159
  399.9 17.3 %fusion.132 = (bf16[3072]{0:T(1024)(128)(2,1)S(1)}, bf16[1024,3072]{1,0:T(8,128)(2,1)}) fusion(f32[1024,3072]{1,0:T(8,128)} %get-tuple-element.313, bf16[1024,768]{1,0:T(8,128)(2,1)S(1)} %bitcast.185, bf16[1,3072,768]{2,1,0:T(8,128)(2,1)} %param.33, f32[1024,3072]{1,0:T(8,128)} %get-tuple-element.324, f32[3072]{0:T(1024)S(1)} %bitcast.221), kind=kOutput, calls=%fused_computation.200 | convolution fusion | flops 4882166784 | bytes 37767168 | tf_op jit(solution)/shard_map/rd,fd->rf/dot_general | solution.py:167
  417.3 8.6 fusion.70
  425.9 40.3 %all_to_all.21 = bf16[8,128,768]{2,1,0:T(8,128)(2,1)} all-to-all(bf16[8,128,768]{2,1,0:T(8,128)(2,1)S(1)} %bitcast.196), channel_id=1, replica_groups=mesh['dp'=8,'head'=4] {'dp'}, dimensions={0} | all-to-all | bytes 3145728 | tf_op jit(solution)/shard_map/all_to_all | solution.py:181
  482.2 22.6 %all-gather.5.cloned.1.call-done = bf16[2048,768]{1,0:T(8,128)(2,1)} async-done(((bf16[512,768]{1,0:T(8,128)(2,1)}), bf16[2048,768]{1,0:T(8,128)(2,1)}) %all-gather.5.cloned.1.call-update) | async-done | bytes 3145744 | tf_op jit(solution)/shard_map/all_gather | solution.py:226
  509.6 124.2 %while.29 = (s32[]{:T(128)}, f32[2048,3,64]{0,2,1:T(8,128)S(1)}, f32[2048,3,64]{0,2,1:T(8,128)}, bf16[4,512,3,64]{1,3,2,0:T(8,128)(2,1)}, s32[4]{0:T(128)S(1)}, ...) while((s32[]{:T(128)}, f32[2048,3,64]{0,2,1:T(8,128)S(1)}, ...), condition=%wide.region_28.29_spmd.clone, body=%wide.region_26.28_spmd.clone.sunk | while | flops 2065759232 | bytes 127140248 | solution.py:266
  656.5 9.8 %fusion.58 = bf16[1,3072,768]{2,1,0:T(8,128)(2,1)} fusion(bf16[1024,3072]{1,0:T(8,128)(2,1)} %copy-done.72, bf16[1024,768]{1,0:T(8,128)(2,1)S(1)} %bitcast.186), kind=kOutput, calls=%fused_computation.83 | convolution fusion | flops 4834197504 | bytes 12582912 | tf_op jit(solution)/shard_map/rf,rd->fd/dot_general | solution.py:170
  666.4 9.3 fusion.57
  689.2 21.3 %all-reduce.2 = bf16[2,3,64]{2,1,0:T(4,128)(2,1)S(1)} all-reduce(bf16[2,3,64]{2,1,0:T(4,128)(2,1)S(1)} %pad_maximum_fusion.3), channel_id=7, replica_groups=mesh['dp'=8,'head'=4] {'dp'}, use_global_device_ids=true, to_apply=%region_39.40.clone | all-reduce | flops 384 | bytes 1536
  712.8 52.3 %reduce-scatter.27.cloned.1.call-done = bf16[96,576]{1,0:T(8,128)(2,1)} async-done(((bf16[768,576]{1,0:T(8,128)(2,1)}), bf16[96,576]{1,0:T(8,128)(2,1)}) %reduce-scatter.27.cloned.1.call-update) | async-done | bytes 110608
  767.2 47.4 %reduce-scatter.25.cloned.1.call-done = bf16[1,768,768]{2,1,0:T(8,128)(2,1)} async-done(((bf16[1,3072,768]{2,1,0:T(8,128)(2,1)}), bf16[1,768,768]{2,1,0:T(8,128)(2,1)}) %reduce-scatter.25.cloned.1.call-update) | async-done | bytes 1179664 | tf_op jit(solution)/shard_map/reduce_scatter | solution.py:195
  817.5 47.6 %reduce-scatter.23.cloned.1.call-done = bf16[1,768,768]{2,1,0:T(8,128)(2,1)} async-done(((bf16[1,768,3072]{2,1,0:T(8,128)(2,1)}), bf16[1,768,768]{2,1,0:T(8,128)(2,1)}) %reduce-scatter.23.cloned.1.call-update) | async-done | bytes 1179664 | tf_op jit(solution)/shard_map/reduce_scatter | solution.py:192
  867.9 37.7 %reduce-scatter.21.cloned.1.call-done = bf16[512,768]{1,0:T(8,128)(2,1)} async-done(((bf16[2048,768]{1,0:T(8,128)(2,1)}), bf16[512,768]{1,0:T(8,128)(2,1)}) %reduce-scatter.21.cloned.1.call-update) | async-done | bytes 786448 | tf_op jit(solution)/shard_map/reduce_scatter | solution.py:285
  907.6 40.1 %all-reduce.7 = (f32[768]{0:T(1024)S(1)}, f32[768]{0:T(1024)S(1)}, f32[768]{0:T(1024)S(1)}, f32[768]{0:T(1024)S(1)}, f32[768]{0:T(1024)S(1)}, /*index=5*/f32[768,8]{0,1:T(8,128)S(1)}) all-reduce(f32[768]{0:T(1024)S(1)} %get-tuple-element.256, f32[768]{0:T(1024)S(1)} %get-tuple-element.260, ...), channel_id=4, replica_groups=mesh['dp'=8,'head'=4] {'dp','head'}, use_global_device_ids=true, to_apply=%region_33.34.clone | all-reduce | flops 9984 | bytes 79872
  (364 shorter events, 309.9 us)
Async XLA Ops:
  7.2 37.4 %all-gather.3.cloned.1.call-start = ((), (), s32[]{:S(2)}) async-start(), calls=%async_computation.12 | async-start | bytes 3932160 | tf_op jit(solution)/shard_map/all_gather | solution.py:50
  13.2 195.9 %reduce-scatter.19.cloned.1.call-start = ((), (), s32[]{:S(2)}) async-start(), calls=%async_computation.13 | async-start | bytes 7864320 | tf_op jit(solution)/shard_map/reduce_scatter | solution.py:102
  216.9 43.1 %all-to-all-start = ((bf16[8,128,768]{2,1,0:T(8,128)(2,1)}), bf16[8,128,768]{2,1,0:T(8,128)(2,1)}, u32[]{:S(2)}, u32[]{:S(2)}) async-start(bf16[8,128,768]{2,1,0:T(8,128)(2,1)} %bitcast.189), calls=%async_computation.1 | async-start | bytes 3145728 | tf_op jit(solution)/shard_map/all_to_all | solution.py:131
  307.2 40.9 %all-to-all-start.1 = ((bf16[8,128,768]{2,1,0:T(8,128)(2,1)}), bf16[8,128,768]{2,1,0:T(8,128)(2,1)}, u32[]{:S(2)}, u32[]{:S(2)}) async-start(bf16[8,128,768]{2,1,0:T(8,128)(2,1)} %bitcast.195), calls=%async_computation.2 | async-start | bytes 3145728 | tf_op jit(solution)/shard_map/all_to_all | solution.py:144
  311.5 193.2 %all-gather.5.cloned.1.call-start = ((), (), s32[]{:S(2)}) async-start(), calls=%async_computation.14 | async-start | bytes 3932160 | tf_op jit(solution)/shard_map/all_gather | solution.py:226
  312.3 158.7 %copy-start.64 = (f32[8]{0:T(128)}, f32[8]{0:T(128)S(1)}, u32[]{:S(2)}) copy-start(f32[8]{0:T(128)S(1)} %broadcast_multiply_fusion.6) | copy-start | bytes 100
  313.8 157.1 %copy-start.26 = (f32[512,8]{0,1:T(8,128)}, f32[512,8]{0,1:T(8,128)S(1)}, u32[]{:S(2)}) copy-start(f32[512,8]{0,1:T(8,128)S(1)} %get-tuple-element.326) | copy-start | bytes 49156
  313.8 157.1 %copy-start.41 = (f32[512]{0:T(512)}, f32[512]{0:T(512)S(1)}, u32[]{:S(2)}) copy-start(f32[512]{0:T(512)S(1)} %get-tuple-element.325) | copy-start | bytes 6148
  313.9 157.1 %copy-start.51 = (f32[512]{0:T(512)}, f32[512]{0:T(512)S(1)}, u32[]{:S(2)}) copy-start(f32[512]{0:T(512)S(1)} %fusion.111) | copy-start | bytes 6148
  478.0 207.8 %reduce-scatter.33.cloned.1.call-start = ((), (), s32[]{:S(2)}) async-start(), calls=%async_computation.21 | async-start | bytes 245760
  480.6 206.7 %reduce-scatter.31.cloned.1.call-start = ((), (), s32[]{:S(2)}) async-start(), calls=%async_computation.20 | async-start | bytes 983040
  482.1 229.0 %reduce-scatter.29.cloned.1.call-start = ((), (), s32[]{:S(2)}) async-start(), calls=%async_computation.19 | async-start | bytes 442368
  637.9 127.2 %reduce-scatter.27.cloned.1.call-start = ((), (), s32[]{:S(2)}) async-start(), calls=%async_computation.18 | async-start | bytes 1105920
  656.4 158.3 %reduce-scatter.25.cloned.1.call-start = ((), (), s32[]{:S(2)}) async-start(), calls=%async_computation.17 | async-start | bytes 5898240 | tf_op jit(solution)/shard_map/reduce_scatter | solution.py:195
  666.3 198.8 %reduce-scatter.23.cloned.1.call-start = ((), (), s32[]{:S(2)}) async-start(), calls=%async_computation.16 | async-start | bytes 5898240 | tf_op jit(solution)/shard_map/reduce_scatter | solution.py:192
  675.8 229.8 %reduce-scatter.21.cloned.1.call-start = ((), (), s32[]{:S(2)}) async-start(), calls=%async_computation.15 | async-start | bytes 3932160 | tf_op jit(solution)/shard_map/reduce_scatter | solution.py:285
  711.2 194.5 %copy-start.7 = (bf16[512,768]{1,0:T(8,128)(2,1)S(1)}, bf16[512,768]{1,0:T(8,128)(2,1)}, u32[]{:S(2)}) copy-start(bf16[512,768]{1,0:T(8,128)(2,1)} %param.21) | copy-start | bytes 2359300
  711.2 194.5 %copy-start.40 = (f32[512]{0:T(512)S(1)}, f32[512]{0:T(512)}, u32[]{:S(2)}) copy-start(f32[512]{0:T(512)} %copy-done.39) | copy-start | bytes 6148
  711.2 194.5 %copy-start.46 = (f32[768]{0:T(1024)S(1)}, f32[768]{0:T(1024)}, u32[]{:S(2)}) copy-start(f32[768]{0:T(1024)} %param.22) | copy-start | bytes 9220
  711.2 194.5 %copy-start.48 = (f32[512]{0:T(512)S(1)}, f32[512]{0:T(512)}, u32[]{:S(2)}) copy-start(f32[512]{0:T(512)} %copy-done.47) | copy-start | bytes 6148
  767.2 140.4 %copy-start.61 = (f32[768]{0:T(1024)S(1)}, f32[768]{0:T(1024)}, u32[]{:S(2)}) copy-start(f32[768]{0:T(1024)} %get-tuple-element.310) | copy-start | bytes 9220
  767.2 184.1 %copy-start.11 = (f32[512,768]{1,0:T(8,128)S(1)}, f32[512,768]{1,0:T(8,128)}, u32[]{:S(2)}) copy-start(f32[512,768]{1,0:T(8,128)} %reduce-scatter.19.cloned.1.call-done) | copy-start | bytes 4718596
  767.2 184.1 %copy-start.38 = (f32[768]{0:T(1024)S(1)}, f32[768]{0:T(1024)}, u32[]{:S(2)}) copy-start(f32[768]{0:T(1024)} %param.27) | copy-start | bytes 9220
  767.2 184.1 %copy-start.58 = (f32[512]{0:T(512)S(1)}, f32[512]{0:T(512)}, u32[]{:S(2)}) copy-start(f32[512]{0:T(512)} %copy-done.57) | copy-start | bytes 6148
  (73 other events, 1733.2 us)
Sparse Core Ops, SparseCore 0:
  13.3 31.2 all-gather.2
  150.6 58.3 reduce-scatter.18
  478.1 26.5 all-gather.4
  507.7 19.7 reduce-scatter.32
  530.1 23.3 reduce-scatter.30
  638.0 61.3 reduce-scatter.28
  702.7 62.3 reduce-scatter.26
  767.8 46.8 reduce-scatter.24
  817.2 47.8 reduce-scatter.22
  867.6 37.9 reduce-scatter.20
where the time goes:
time: 969 us; the launch traced here: 964 us
  waiting for transfers between devices  365 us (38%)
  matrix products  253 us (26%)
  blocking collectives  143 us (15%)
  other arithmetic  111 us (11%)
  local copies, waits for them, and re-layouts  49.5 us (5%)
  between operations  17.7 us (2%)
  loops' own time  14.4 us (1%)
  starting transfers between devices  11 us (1%)
    unnamed x2, blocking collectives  61.4 us
    reduce_scatter x1, waiting for transfers between devices, local(): lax.psum_scatter(jnp.dot(piece, proj_weight, preferred_element_type=jnp.f...  56.3 us
    unnamed x14, waiting for transfers between devices  52.5 us
    reduce_scatter x1, waiting for transfers between devices, local(): lax.psum_scatter(up_grad[None].astype(jnp.bfloat16), 'head', scatter_dime...  47.6 us
    reduce_scatter x1, waiting for transfers between devices, local(): lax.psum_scatter(down_grad[None].astype(jnp.bfloat16), 'head', scatter_di...  47.4 us
    all_to_all x1, blocking collectives, local(): lax.all_to_all(send_grads.reshape(num_experts, capacity, width), 'dp', sp...  40.9 us
    all_to_all x1, blocking collectives, local(): lax.all_to_all(grad_rows.reshape(num_experts, capacity, width), 'dp', spl...  40.3 us
    reduce_scatter x1, waiting for transfers between devices, local(): lax.psum_scatter(jnp.einsum('cte,cde->td', piece, qkv_weight, preferred_e...  37.7 us
  transfers between devices with their start and end apart: 12, of which 9 were waited for; matrix products, arithmetic and copies ran while one was open for 20% of the time, Pallas kernels for 0%

commit v1 on v0

--- a/solution.py
+++ b/solution.py
@@ -1,12 +1,39 @@
+import functools
 import jax
 import jax.numpy as jnp
 from jax import lax
+from jax.experimental import pallas as pl
+from jax.experimental.pallas import tpu as pltpu
 from jax.sharding import PartitionSpec as P
 
 EPSILON = 1e-05
 BAL_COEF = 0.01
 HIGHEST = lax.Precision.HIGHEST
 NEG_LARGE = -1e30
+MESH = pl.DeviceIdType.MESH
+F32 = jnp.float32
+BF16 = jnp.bfloat16
+TILE = 256
+VMEM_LIMIT = 60 << 20
+
+
+def flip(index, bits):
+    out, bit = index, 1
+    while bit <= bits:
+        if bits & bit:
+            out = out + bit - 2 * bit * lax.rem(lax.div(index, bit), 2)
+        bit *= 2
+    return out
+
+
+def remote(src, dst, send_sem, recv_sem, device):
+    return pltpu.make_async_remote_copy(
+        src_ref=src, dst_ref=dst, send_sem=send_sem, recv_sem=recv_sem, device_id=device, device_id_type=MESH
+    )
+
+
+def dot(left, right, dims=((1,), (0,)), precision=None):
+    return lax.dot_general(left, right, (dims, ((), ())), precision=precision, preferred_element_type=F32)
 
 
 def normalize(values, gain, bias):
@@ -23,6 +50,256 @@
     first_mean = jnp.mean(grad_scaled, axis=-1, keepdims=True)
     second_mean = jnp.mean(grad_scaled * scaled, axis=-1, keepdims=True)
     return inverse * (grad_scaled - first_mean - scaled * second_mean)
+
+
+def slot_layouts(routes, experts, cap):
+    rows = routes.shape[1]
+    count = max(8, experts)
+    expert = lax.broadcasted_iota(jnp.int32, (count, rows), 0)
+    hot = (routes == expert).astype(F32)
+    upto = lax.broadcasted_iota(jnp.int32, (rows, rows), 0) <= lax.broadcasted_iota(jnp.int32, (rows, rows), 1)
+    rank = dot(hot.astype(BF16), upto.astype(F32).astype(BF16))
+    slot_row = jnp.sum((rank - 1.0) * hot, axis=0, keepdims=True)
+    flat_row = jnp.sum((rank - 1.0 + cap * expert.astype(F32)) * hot, axis=0, keepdims=True)
+    return hot, flat_row.astype(jnp.int32), slot_row.astype(jnp.int32)
+
+
+def barrier_signal(peers):
+    barrier = pltpu.get_barrier_semaphore()
+    for peer in peers:
+        pl.semaphore_signal(barrier, inc=1, device_id=peer, device_id_type=MESH)
+
+
+def barrier_wait(count):
+    pl.semaphore_wait(pltpu.get_barrier_semaphore(), count)
+
+
+def kernel_a(
+    n_dp, x_ref, g1_ref, b1_ref, w_ref, qb_ref, proj_ref, routes_ref, cot_ref, len_ref,
+    gath_o, qkv_o, p_o, ctx_o, ctxf_o, projf_o, cots_o,
+    gath, qkv, p_st, bias_s, ctx_s, disp,
+    ag_s, ag_r, pj_s, pj_r, cx_s, cx_r, ct_s, ct_r, p_sem, loc,
+):
+    tok, width = x_ref.shape
+    heads = qb_ref.shape[0]
+    hd = qb_ref.shape[2]
+    group = 4 * tok
+    tiles = group // TILE
+    reach = group // 2 // TILE + 1
+    cap = cots_o.shape[0] // n_dp
+    d = lax.axis_index("dp")
+    h = lax.axis_index("head")
+    barrier_signal([(d, flip(h, k)) for k in (1, 2, 3)] + [(flip(d, r), h) for r in range(1, n_dp)])
+
+    normed, _, _ = normalize(x_ref[...].astype(F32), g1_ref[...][None, :], b1_ref[...][None, :])
+
+    def block(index):
+        return pl.ds(pl.multiple_of(index * tok, tok), tok)
+
+    gath[block(h), :] = normed.astype(BF16)
+    barrier_wait(3 + n_dp - 1)
+
+    chunks = 4
+    step = tok // chunks
+
+    def part(index, i):
+        return gath.at[pl.ds(pl.multiple_of(index * tok + i * step, step), step), :]
+
+    sib, cross, diag = flip(h, 1), flip(h, 2), flip(h, 3)
+    to_cross = [remote(part(h, i), part(h, i), ag_s.at[i], ag_r.at[i], (d, cross)) for i in range(chunks)]
+    to_sib = remote(gath.at[block(h), :], gath.at[block(h), :], ag_s.at[2 * chunks], ag_r.at[2 * chunks], (d, sib))
+    onward = [
+        remote(part(cross, i), part(cross, i), ag_s.at[chunks + i], ag_r.at[chunks + i], (d, sib)) for i in range(chunks)
+    ]
+    for copy in to_cross:
+        copy.start()
+    to_sib.start()
+    proj_copies = [
+        remote(proj_ref, projf_o.at[h], pj_s.at[k], pj_r.at[k], (d, flip(h, k))) for k in (1, 2, 3)
+    ]
+
+    hot_t, flat_row, slot_row = slot_layouts(routes_ref[...], n_dp, cap)
+    slot_iota = lax.broadcasted_iota(jnp.int32, (cap, tok), 0)
+
+    def dispatch(e, carry):
+        hot = (flat_row == slot_iota + e * cap).astype(F32).astype(BF16)
+        disp[pl.ds(pl.multiple_of(e * cap, cap), cap), :] = dot(hot, cot_ref[...]).astype(BF16)
+        return carry
+
+    lax.fori_loop(0, n_dp, dispatch, 0)
+
+    def slots(index):
+        return pl.ds(pl.multiple_of(index * cap, cap), cap)
+
+    cot_copies = [
+        remote(disp.at[slots(flip(d, r)), :], cots_o.at[pl.ds(r * cap, cap), :], ct_s.at[r], ct_r.at[r], (flip(d, r), h))
+        for r in range(1, n_dp)
+    ]
+    for copy in cot_copies:
+        copy.start()
+    cot_own = pltpu.make_async_copy(disp.at[slots(d), :], cots_o.at[pl.ds(0, cap), :], ct_s.at[0])
+    cot_own.start()
+
+    def project(index):
+        rows = gath[block(index), :]
+        for c in range(3):
+            out = dot(rows, w_ref[c], ((1,), (1,)))
+            for a in range(heads):
+                piece = out[:, a * hd : (a + 1) * hd]
+                if c != 1:
+                    piece = piece + qb_ref[a, c // 2 : c // 2 + 1, :]
+                piece = piece.astype(BF16)
+                if c == 0:
+                    piece = piece * jnp.asarray(hd ** (-0.5), BF16)
+                qkv[c, a, block(index), :] = piece
+
+    project(h)
+    to_sib.wait_recv()
+    project(sib)
+    for i in range(chunks):
+        to_cross[i].wait_recv()
+        onward[i].start()
+    for copy in proj_copies:
+        copy.start()
+    proj_own = pltpu.make_async_copy(proj_ref, projf_o.at[h], loc.at[0])
+    proj_own.start()
+    project(cross)
+    for i in range(chunks):
+        onward[i].wait_recv()
+    project(diag)
+    gath_copy = pltpu.make_async_copy(gath, gath_o, loc.at[1])
+    gath_copy.start()
+    qkv_copy = pltpu.make_async_copy(qkv, qkv_o, loc.at[2])
+    qkv_copy.start()
+
+    ends = [len_ref[0, 0]]
+    for i in range(1, len_ref.shape[1] - 1):
+        ends.append(ends[-1] + len_ref[0, i])
+
+    order = []
+    for i in range(tiles // 2):
+        order += [tiles - 1 - i, tiles // 2 - 1 - i]
+    per_block = tok // TILE
+
+    def p_copy(t, a):
+        size = min(t + 1, reach) * TILE
+        return pltpu.make_async_copy(p_st.at[a, :, pl.ds(0, size)], p_o.at[a, t, :, pl.ds(0, size)], p_sem.at[a])
+
+    previous = None
+    for t in order:
+        size = min(t + 1, reach) * TILE
+        first = (t + 1) * TILE - size
+        row = t * TILE + lax.broadcasted_iota(jnp.int32, (TILE, 1), 0)
+        start = jnp.zeros((TILE, 1), jnp.int32)
+        for end in ends:
+            start = jnp.where(row >= end, end, start)
+        col = first + lax.broadcasted_iota(jnp.int32, (TILE, size), 1)
+        bias_s[:, :size] = jnp.where((col >= start) & (col <= row), 0.0, NEG_LARGE)
+        outs = []
+        for a in range(heads):
+            q = qkv[0, a, t * TILE : (t + 1) * TILE, :]
+            k = qkv[1, a, first : (t + 1) * TILE, :]
+            v = qkv[2, a, first : (t + 1) * TILE, :]
+            s = dot(q, k, ((1,), (1,))) + bias_s[:, :size]
+            top = jnp.max(s, axis=1, keepdims=True)
+            e = jnp.exp(s - top)
+            total = jnp.sum(e, axis=1, keepdims=True)
+            p = (e * (1.0 / total)).astype(BF16)
+            if previous is not None:
+                p_copy(previous, a).wait()
+            p_st[a, :, :size] = p
+            p_copy(t, a).start()
+            outs.append(dot(p, v))
+        ctx_s[t] = jnp.concatenate(outs, axis=1).astype(BF16)
+        previous = t
+        owner, sub = t // per_block, t % per_block
+        rows = pl.ds(sub * TILE, TILE)
+
+        @pl.when(h != owner)
+        def _():
+            remote(ctx_s.at[t], ctxf_o.at[h, rows, :], cx_s.at[t], cx_r.at[h, sub], (d, owner)).start()
+
+        @pl.when(h == owner)
+        def _():
+            pltpu.make_async_copy(ctx_s.at[t], ctxf_o.at[h, rows, :], cx_s.at[t]).start()
+
+    ctx_copy = pltpu.make_async_copy(ctx_s, ctx_o, loc.at[3])
+    ctx_copy.start()
+    for a in range(heads):
+        p_copy(previous, a).wait()
+    for t in range(tiles):
+        owner, sub = t // per_block, t % per_block
+        rows = pl.ds(sub * TILE, TILE)
+
+        @pl.when(h != owner)
+        def _():
+            remote(ctx_s.at[t], ctxf_o.at[h, rows, :], cx_s.at[t], cx_r.at[h, sub], (d, owner)).wait_send()
+
+        @pl.when(h == owner)
+        def _():
+            pltpu.make_async_copy(ctx_s.at[t], ctxf_o.at[h, rows, :], cx_s.at[t]).wait()
+
+    for k in (1, 2, 3):
+        peer = flip(h, k)
+        for sub in range(per_block):
+            remote(
+                ctx_s.at[0], ctxf_o.at[peer, pl.ds(sub * TILE, TILE), :], cx_s.at[0], cx_r.at[peer, sub], (d, peer)
+            ).wait_recv()
+    for copy in to_cross:
+        copy.wait_send()
+    to_sib.wait_send()
+    for copy in onward:
+        copy.wait_send()
+    for k in (1, 2, 3):
+        proj_copies[k - 1].wait_send()
+        peer = flip(h, k)
+        remote(proj_ref, projf_o.at[peer], pj_s.at[k], pj_r.at[k], (d, peer)).wait_recv()
+    for copy in cot_copies:
+        copy.wait()
+    for copy in (cot_own, proj_own, gath_copy, qkv_copy, ctx_copy):
+        copy.wait()
+
+
+VM = pl.BlockSpec(memory_space=pltpu.VMEM)
+SM = pl.BlockSpec(memory_space=pltpu.SMEM)
+ANY = pl.BlockSpec(memory_space=pl.ANY)
+DMA = pltpu.SemaphoreType.DMA
+
+
+def stage_a(n_dp, x, g1, b1, w, qb, proj, routes, cot, lengths, cap):
+    tok, width = x.shape
+    heads, hd = qb.shape[1:]
+    w, qb, routes = w.transpose(0, 2, 1), qb.transpose(1, 0, 2), routes.T
+    group = 4 * tok
+    tiles = group // TILE
+    span = (group // 2 // TILE + 1) * TILE
+    cols = heads * hd
+    sds = jax.ShapeDtypeStruct
+    return pl.pallas_call(
+        functools.partial(kernel_a, n_dp),
+        out_shape=(
+            sds((group, width), BF16),
+            sds((3, heads, group, hd), BF16),
+            sds((heads, tiles, TILE, span), BF16),
+            sds((tiles, TILE, cols), BF16),
+            sds((4, tok, cols), BF16),
+            sds((4, cols, width), BF16),
+            sds((n_dp * cap, width), BF16),
+        ),
+        in_specs=[VM] * 8 + [SM],
+        out_specs=(ANY,) * 7,
+        scratch_shapes=[
+            pltpu.VMEM((group, width), BF16),
+            pltpu.VMEM((3, heads, group, hd), BF16),
+            pltpu.VMEM((heads, TILE, span), BF16),
+            pltpu.VMEM((TILE, span), F32),
+            pltpu.VMEM((tiles, TILE, cols), BF16),
+            pltpu.VMEM((n_dp * cap, width), BF16),
+            DMA((9,)), DMA((9,)), DMA((4,)), DMA((4,)), DMA((tiles,)), DMA((4, tok // TILE)),
+            DMA((n_dp,)), DMA((n_dp,)), DMA((heads,)), DMA((4,)),
+        ],
+        compiler_params=pltpu.CompilerParams(collective_id=0, has_side_effects=True, vmem_limit_bytes=VMEM_LIMIT),
+    )(x, g1, b1, w, qb, proj, routes, cot, lengths)
 
 
 def local(
@@ -47,16 +324,18 @@
     tok_rows, width = block_input.shape
     input_float = block_input.astype(jnp.float32)
     normed_one, scaled_one, inverse_one = normalize(input_float, norm1_gain, norm1_bias)
-    gathered = lax.all_gather(normed_one.astype(jnp.bfloat16), "head", axis=0, tiled=True)
+    num_experts = router_weight.shape[1]
+    capacity = 2 * tok_rows // num_experts
+    gathered, qkv_heads, kept_probs, context_tiles, context_full, proj_full, cot_slots = stage_a(
+        num_experts, block_input, norm1_gain, norm1_bias, qkv_weight, qkv_bias, proj_weight, routes, cotangent, lengths, capacity
+    )
     group_rows = gathered.shape[0]
     local_heads = qkv_bias.shape[1]
     head_size = qkv_bias.shape[2]
     local_cols = local_heads * head_size
     head_shape = (group_rows, local_heads, head_size)
-    projected = jnp.einsum("td,cde->cte", gathered, qkv_weight, preferred_element_type=jnp.float32)
-    queries = (projected[0] + qkv_bias[0].reshape(-1)).astype(jnp.bfloat16).reshape(head_shape)
-    keys_all = projected[1].astype(jnp.bfloat16).reshape(head_shape)
-    values_all = (projected[2] + qkv_bias[1].reshape(-1)).astype(jnp.bfloat16).reshape(head_shape)
+    context = context_tiles.reshape(group_rows, local_cols)
+    queries, keys_all, values_all = (qkv_heads[i].transpose(1, 0, 2) for i in range(3))
     positions = jnp.arange(group_rows, dtype=jnp.int32)
     seq_ends = jnp.cumsum(lengths[0])
     segment = jnp.sum((positions[:, None] >= seq_ends[None, :]).astype(jnp.int32), axis=1)
@@ -71,44 +350,12 @@
         allowed = (seg_block[:, None] == segment[None, :]) & (
             positions[None, :] <= pos_block[:, None]
         )
-        scores = (
-            jnp.einsum("qhd,khd->hqk", query_block, keys_all, preferred_element_type=jnp.float32)
-            * score_scale
-        )
+        scores = jnp.einsum("qhd,khd->hqk", query_block, keys_all, preferred_element_type=jnp.float32)
         return (query_block, jnp.where(allowed[None], scores, NEG_LARGE))
 
-    def attend_block(state_in, block_index):
-        query_block, scores = block_scores(block_index * block_rows)
-        row_max = jnp.max(scores, axis=-1, keepdims=True)
-        exponent = jnp.exp(scores - row_max)
-        row_total = jnp.sum(exponent, axis=-1, keepdims=True)
-        probability = exponent / row_total
-        context_block = jnp.einsum(
-            "hqk,khd->qhd",
-            probability.astype(jnp.bfloat16),
-            values_all,
-            preferred_element_type=jnp.float32,
-        )
-        return (
-            state_in,
-            (context_block.astype(jnp.bfloat16), (row_max + jnp.log(row_total))[..., 0]),
-        )
-
-    unused_state, (context_blocks, lse_blocks) = lax.scan(
-        attend_block, jnp.zeros((), jnp.float32), jnp.arange(blocks)
-    )
-    context = context_blocks.reshape(group_rows, local_cols)
-    piece = context
-    attended = lax.psum_scatter(
-        jnp.dot(piece, proj_weight, preferred_element_type=jnp.float32),
-        "head",
-        scatter_dimension=0,
-        tiled=True,
-    )
+    attended = jnp.einsum("hrc,hcd->rd", context_full, proj_full, preferred_element_type=jnp.float32)
     residual = input_float + attended + proj_bias
     normed_two, scaled_two, inverse_two = normalize(residual, norm2_gain, norm2_bias)
-    num_experts = router_weight.shape[1]
-    capacity = 2 * tok_rows // num_experts
     logits = jnp.dot(
         normed_two, router_weight, precision=HIGHEST, preferred_element_type=jnp.float32
     )
@@ -153,16 +400,13 @@
     grad_out = cotangent.astype(jnp.float32)
     grad_gate = jnp.sum(grad_out * expert_out, axis=1)
     grad_produced = (gate_value[:, None] * grad_out).astype(jnp.bfloat16)
-    send_grads = (
-        jnp.zeros((num_experts * capacity, width), jnp.bfloat16).at[flat_index].set(grad_produced)
-    )
-    grads_in = lax.all_to_all(
-        send_grads.reshape(num_experts, capacity, width),
-        "dp",
-        split_axis=0,
-        concat_axis=0,
-        tiled=True,
-    ).reshape(num_experts * capacity, width)
+    send_gates = jnp.zeros((num_experts * capacity,), jnp.float32).at[flat_index].set(gate_value)
+    gates_in = lax.all_to_all(
+        send_gates.reshape(num_experts, capacity), "dp", split_axis=0, concat_axis=0, tiled=True
+    )
+    order = jnp.arange(num_experts, dtype=jnp.int32) ^ lax.axis_index("dp")
+    cots_in = cot_slots.reshape(num_experts, capacity, width)[order]
+    grads_in = (gates_in[:, :, None] * cots_in.astype(jnp.float32)).astype(jnp.bfloat16).reshape(num_experts * capacity, width)
     preact_back, hidden_back = (preact_out, hidden)
     grad_hidden = jnp.einsum(
         "rd,fd->rf", grads_in, down_weight[0], preferred_element_type=jnp.float32
@@ -235,8 +479,7 @@
         grad_keys, grad_values = state_in
         first_row = block_index * block_rows
         query_block, scores = block_scores(first_row)
-        lse_block = lse_blocks[block_index]
-        prob_block = jnp.exp(scores - lse_block[..., None])
+        prob_block = jax.nn.softmax(scores, axis=-1)
         grad_ctx_block = lax.dynamic_slice_in_dim(grad_context, first_row, block_rows, 0)
         grad_prob_block = jnp.einsum(
             "qhd,khd->hqk", grad_ctx_block, values_all, preferred_element_type=jnp.float32
@@ -252,7 +495,6 @@
             + jnp.einsum(
                 "hqk,qhd->khd", grad_scores, query_block, preferred_element_type=jnp.float32
             )
-            * score_scale
         )
         grad_values = grad_values + jnp.einsum(
             "hqk,qhd->khd",

time: 969 us -> 880 us (0.908)
  waiting for transfers between devices: 365 us -> 273 us
  Pallas kernels: 0 us -> 52.9 us
  blocking collectives: 143 us -> 99.9 us
  matrix products: 253 us -> 227 us
  other arithmetic: 111 us -> 129 us
  loops' own time: 14.4 us -> 3.09 us
    sub x0 -> x4, other arithmetic: none -> 69.6 us  [attend_back(): prob_block = jax.nn.softmax(scores, axis=-1)]
    reduce_scatter x1 -> x0, waiting for transfers between devices: 56.3 us -> none  [local(): lax.psum_scatter(jnp.dot(piece, proj_weight, preferred_element_type=jnp.f...]
    pallas_call x0 -> x1, Pallas kernels: none -> 52.9 us  [stage_a(): pl.pallas_call(functools.partial(kernel_a, n_dp), out_shape=(sds((group,...]
    all_to_all x1 -> x0, blocking collectives: 40.9 us -> none  [local(): lax.all_to_all(send_grads.reshape(num_experts, capacity, width), 'dp', sp...]
    dot_general x5 -> x1, matrix products: 33 us -> 2.76 us  [local(): jnp.einsum('hrc,hcd->rd', context_full, proj_full, preferred_element_type...]
    all_gather x1 -> x0, waiting for transfers between devices: 29.7 us -> none  [local(): lax.all_gather(normed_one.astype(jnp.bfloat16), 'head', axis=0, tiled=True)]
    reduce_sum x4 -> x0, other arithmetic: 27.1 us -> none  [attend_block(): row_total = jnp.sum(exponent, axis=-1, keepdims=True)]
    dot_general x4, matrix products: 14.6 us -> 30.7 us  [attend_back(): jnp.einsum('hqk,qhd->khd', prob_block.astype(jnp.bfloat16), grad_ctx_bloc...]
  transfers between devices with their start and end apart: 12 -> 11, of which waited for: 9 -> 8; matrix products, arithmetic and copies ran while one was open for 20% -> 34% of each run, Pallas kernels for 0% -> 0%
where the time goes in v1:
time: 880 us; the launch traced here: 869 us
  waiting for transfers between devices  273 us (31%)
  matrix products  227 us (26%)
  other arithmetic  129 us (15%)
  blocking collectives  99.9 us (11%)
  local copies, waits for them, and re-layouts  54.2 us (6%)
  Pallas kernels  52.9 us (6%)
  between operations  17.9 us (2%)
  starting transfers between devices  11.7 us (1%)
    sub x4, other arithmetic, attend_back(): prob_block = jax.nn.softmax(scores, axis=-1)  69.6 us
    unnamed x2, blocking collectives  61.4 us
    unnamed x12, waiting for transfers between devices  53.9 us
    pallas_call x1, Pallas kernels, stage_a(): pl.pallas_call(functools.partial(kernel_a, n_dp), out_shape=(sds((group,...  52.9 us
    reduce_scatter x1, waiting for transfers between devices, local(): lax.psum_scatter(up_grad[None].astype(jnp.bfloat16), 'head', scatter_dime...  47.7 us
    reduce_scatter x1, waiting for transfers between devices, local(): lax.psum_scatter(down_grad[None].astype(jnp.bfloat16), 'head', scatter_di...  47.2 us
    all_to_all x1, blocking collectives, local(): lax.all_to_all(grad_rows.reshape(num_experts, capacity, width), 'dp', spl...  38.5 us
    reduce_scatter x1, waiting for transfers between devices, local(): lax.psum_scatter(jnp.einsum('cte,cde->td', piece, qkv_weight, preferred_e...  37.7 us
  transfers between devices with their start and end apart: 11, of which 8 were waited for; matrix products, arithmetic and copies ran while one was open for 34% of the time, Pallas kernels for 0%

profile of v1, /device:TPU:0, one launch (start us, length us, event | category | flops | bytes accessed | tf_op | source)
XLA Modules:
  0.0 868.9 jit_solution(13190535345331341972)
XLA Ops:
  7.2 52.9 %shard_map.288 = (bf16[2048,768]{1,0:T(8,128)(2,1)}, bf16[3,3,2048,64]{3,2,1,0:T(8,128)(2,1)}, bf16[3,8,256,1280]{3,2,1,0:T(8,128)(2,1)}, bf16[8,256,192]{2,1,0:...) custom-call(bf16[512,768]{1,0:T(8,128)(2,1)} %x_ref.1, ...), custom_call_target="tpu_custom_call" | custom-call | tf_op jit(solution)/shard_map/pallas_call | solution.py:278
  72.7 35.2 %all-to-all-done = bf16[8,128,768]{2,1,0:T(8,128)(2,1)S(1)} async-done(((bf16[8,128,768]{2,1,0:T(8,128)(2,1)}), bf16[8,128,768]{2,1,0:T(8,128)(2,1)S(1)}, u32[]{:S(2)}, u32[]{:S(2)}) %all-to-all-start) | async-done | bytes 1572896 | tf_op jit(solution)/shard_map/all_to_all | solution.py:378
  107.9 36.0 %multiply_convert_fusion.1 = (bf16[1024,3072]{1,0:T(8,128)(2,1)S(1)}, f32[1024,3072]{1,0:T(8,128)}, f32[1024,3072]{1,0:T(8,128)}) fusion(f32[3072]{0:T(1024)S(1)} %bitcast.198, bf16[1024,768]{1,0:T(8,128)(2,1)S(1)} %bitcast.163, bf16[1,768,3072]{2,1,0:T(8,128)(2,1)} %param.29), kind=kOutput, calls=%fused_computation.42 | convolution fusion | flops 5039456256 | bytes 37761024 | tf_op jit(solution)/shard_map/dot_general | solution.py:386
  144.0 10.7 %add_convert_fusion.1 = bf16[1024,768]{1,0:T(8,128)(2,1)} fusion(bf16[1024,3072]{1,0:T(8,128)(2,1)S(1)} %get-tuple-element.272, bf16[1,3072,768]{2,1,0:T(8,128)(2,1)} %param.31, f32[768]{0:T(1024)S(1)} %reduce.8), kind=kOutput, calls=%fused_computation.73 | convolution fusion | flops 4833411072 | bytes 12585984 | tf_op jit(solution)/shard_map/dot_general | solution.py:389
  160.6 35.0 %all-to-all-done.1 = bf16[8,128,768]{2,1,0:T(8,128)(2,1)S(1)} async-done(((bf16[8,128,768]{2,1,0:T(8,128)(2,1)}), bf16[8,128,768]{2,1,0:T(8,128)(2,1)S(1)}, u32[]{:S(2)}, u32[]{:S(2)}) %all-to-all-start.1) | async-done | bytes 1572896 | tf_op jit(solution)/shard_map/all_to_all | solution.py:391
  214.0 17.2 %fusion.116 = (bf16[3072]{0:T(1024)(128)(2,1)S(1)}, bf16[1024,3072]{1,0:T(8,128)(2,1)}) fusion(f32[1024,3072]{1,0:T(8,128)} %get-tuple-element.273, bf16[1024,768]{1,0:T(8,128)(2,1)S(1)} %bitcast.169, bf16[1,3072,768]{2,1,0:T(8,128)(2,1)} %param.31, f32[1024,3072]{1,0:T(8,128)} %get-tuple-element.284, f32[3072]{0:T(1024)S(1)} %bitcast.199), kind=kOutput, calls=%fused_computation.182 | convolution fusion | flops 4882166784 | bytes 37767168 | tf_op jit(solution)/shard_map/rd,fd->rf/dot_general | solution.py:411
  231.2 8.6 fusion.58
  239.8 38.5 %all_to_all.24 = bf16[8,128,768]{2,1,0:T(8,128)(2,1)S(1)} all-to-all(bf16[8,128,768]{2,1,0:T(8,128)(2,1)S(1)} %bitcast.166), channel_id=1, replica_groups=mesh['dp'=8,'head'=4] {'dp'}, dimensions={0} | all-to-all | bytes 3145728 | tf_op jit(solution)/shard_map/all_to_all | solution.py:425
  305.3 12.2 %all-gather.2.cloned.1.call-done = bf16[2048,768]{1,0:T(8,128)(2,1)} async-done(((bf16[512,768]{1,0:T(8,128)(2,1)}), bf16[2048,768]{1,0:T(8,128)(2,1)}) %all-gather.2.cloned.1.call-update) | async-done | bytes 3145744 | tf_op jit(solution)/shard_map/all_gather | solution.py:470
  321.4 218.1 %while.15 = (s32[]{:T(128)}, f32[2048,3,64]{0,2,1:T(8,128)S(1)}, f32[2048,3,64]{0,2,1:T(8,128)}, bf16[4,512,3,64]{1,3,2,0:T(8,128)(2,1)}, s32[4]{0:T(128)S(1)}, ...) while((s32[]{:T(128)}, f32[2048,3,64]{0,2,1:T(8,128)S(1)}, ...), condition=%wide.region_25.26_spmd.clone, body=%wide.region_21.25_spmd.clone.sunk | while | flops 2059076608 | bytes 184802080 | solution.py:508
  331.4 17.4 %fusion.165 = (f32[3,512]{1,0:T(4,128)S(1)}, f32[3,512,2048]{2,1,0:T(8,128)}) fusion(f32[3,512,2048]{2,1,0:T(8,128)} %fusion.163, pred[512,2048]{1,0:T(8,128)(4,1)S(1)} %fusion.164), kind=kOutput, calls=%fused_computation.179.clone.1 | output fusion | flops 12584959 | bytes 26220544 | tf_op jit(solution)/shard_map/while/body/eval_jaxpr/sub | solution.py:482
  385.8 17.4 %fusion.165 = (f32[3,512]{1,0:T(4,128)S(1)}, f32[3,512,2048]{2,1,0:T(8,128)}) fusion(f32[3,512,2048]{2,1,0:T(8,128)} %fusion.163, pred[512,2048]{1,0:T(8,128)(4,1)S(1)} %fusion.164), kind=kOutput, calls=%fused_computation.179.clone.1 | output fusion | flops 12584959 | bytes 26220544 | tf_op jit(solution)/shard_map/while/body/eval_jaxpr/sub | solution.py:482
  403.2 7.7 fusion.167
  440.3 17.4 %fusion.165 = (f32[3,512]{1,0:T(4,128)S(1)}, f32[3,512,2048]{2,1,0:T(8,128)}) fusion(f32[3,512,2048]{2,1,0:T(8,128)} %fusion.163, pred[512,2048]{1,0:T(8,128)(4,1)S(1)} %fusion.164), kind=kOutput, calls=%fused_computation.179.clone.1 | output fusion | flops 12584959 | bytes 26220544 | tf_op jit(solution)/shard_map/while/body/eval_jaxpr/sub | solution.py:482
  494.7 17.4 %fusion.165 = (f32[3,512]{1,0:T(4,128)S(1)}, f32[3,512,2048]{2,1,0:T(8,128)}) fusion(f32[3,512,2048]{2,1,0:T(8,128)} %fusion.163, pred[512,2048]{1,0:T(8,128)(4,1)S(1)} %fusion.164), kind=kOutput, calls=%fused_computation.179.clone.1 | output fusion | flops 12584959 | bytes 26220544 | tf_op jit(solution)/shard_map/while/body/eval_jaxpr/sub | solution.py:482
  512.1 7.7 fusion.167
  558.6 9.1 %fusion.46 = bf16[1,3072,768]{2,1,0:T(8,128)(2,1)} fusion(bf16[1024,3072]{1,0:T(8,128)(2,1)} %copy-done.60, bf16[1024,768]{1,0:T(8,128)(2,1)} %fusion.47), kind=kOutput, calls=%fused_computation.67 | convolution fusion | flops 4834197504 | bytes 12582912 | tf_op jit(solution)/shard_map/rf,rd->fd/dot_general | solution.py:414
  569.2 9.6 %fusion.45 = bf16[1,768,3072]{2,1,0:T(8,128)(2,1)} fusion(bf16[1024,768]{1,0:T(8,128)(2,1)S(1)} %bitcast.164, bf16[1024,3072]{1,0:T(8,128)(2,1)} %get-tuple-element.289), kind=kOutput, calls=%fused_computation.66 | convolution fusion | flops 4834197504 | bytes 12582912 | tf_op jit(solution)/shard_map/rd,rf->df/dot_general | solution.py:420
  594.3 21.4 %all-reduce.2 = bf16[2,3,64]{2,1,0:T(4,128)(2,1)S(1)} all-reduce(bf16[2,3,64]{2,1,0:T(4,128)(2,1)S(1)} %pad_maximum_fusion.3), channel_id=6, replica_groups=mesh['dp'=8,'head'=4] {'dp'}, use_global_device_ids=true, to_apply=%region_36.37.clone | all-reduce | flops 384 | bytes 1536
  617.9 53.7 %reduce-scatter.24.cloned.1.call-done = bf16[96,576]{1,0:T(8,128)(2,1)} async-done(((bf16[768,576]{1,0:T(8,128)(2,1)}), bf16[96,576]{1,0:T(8,128)(2,1)}) %reduce-scatter.24.cloned.1.call-update) | async-done | bytes 110608
  673.7 47.2 %reduce-scatter.22.cloned.1.call-done = bf16[1,768,768]{2,1,0:T(8,128)(2,1)} async-done(((bf16[1,3072,768]{2,1,0:T(8,128)(2,1)}), bf16[1,768,768]{2,1,0:T(8,128)(2,1)}) %reduce-scatter.22.cloned.1.call-update) | async-done | bytes 1179664 | tf_op jit(solution)/shard_map/reduce_scatter | solution.py:439
  723.8 47.7 %reduce-scatter.20.cloned.1.call-done = bf16[1,768,768]{2,1,0:T(8,128)(2,1)} async-done(((bf16[1,768,3072]{2,1,0:T(8,128)(2,1)}), bf16[1,768,768]{2,1,0:T(8,128)(2,1)}) %reduce-scatter.20.cloned.1.call-update) | async-done | bytes 1179664 | tf_op jit(solution)/shard_map/reduce_scatter | solution.py:436
  774.3 37.7 %reduce-scatter.18.cloned.1.call-done = bf16[512,768]{1,0:T(8,128)(2,1)} async-done(((bf16[2048,768]{1,0:T(8,128)(2,1)}), bf16[512,768]{1,0:T(8,128)(2,1)}) %reduce-scatter.18.cloned.1.call-update) | async-done | bytes 786448 | tf_op jit(solution)/shard_map/reduce_scatter | solution.py:527
  814.0 40.1 %all-reduce.7 = (f32[768]{0:T(1024)S(1)}, f32[768]{0:T(1024)S(1)}, f32[768]{0:T(1024)S(1)}, f32[768]{0:T(1024)S(1)}, f32[768]{0:T(1024)S(1)}, /*index=5*/f32[768,8]{0,1:T(8,128)S(1)}) all-reduce(f32[768]{0:T(1024)S(1)} %get-tuple-element.232, f32[768]{0:T(1024)S(1)} %get-tuple-element.236, ...), channel_id=3, replica_groups=mesh['dp'=8,'head'=4] {'dp','head'}, use_global_device_ids=true, to_apply=%region_30.31.clone | all-reduce | flops 9984 | bytes 79872
  (283 shorter events, 250.1 us)
Async XLA Ops:
  7.2 151.5 %copy-start = (f32[768,8]{0,1:T(8,128)S(1)}, f32[768,8]{0,1:T(8,128)}, u32[]{:S(2)}) copy-start(f32[768,8]{0,1:T(8,128)} %param.28) | copy-start | bytes 73732
  68.8 39.1 %all-to-all-start = ((bf16[8,128,768]{2,1,0:T(8,128)(2,1)}), bf16[8,128,768]{2,1,0:T(8,128)(2,1)S(1)}, u32[]{:S(2)}, u32[]{:S(2)}) async-start(bf16[8,128,768]{2,1,0:T(8,128)(2,1)} %bitcast.10), calls=%async_computation | async-start | bytes 3145728 | tf_op jit(solution)/shard_map/all_to_all | solution.py:378
  154.8 40.8 %all-to-all-start.1 = ((bf16[8,128,768]{2,1,0:T(8,128)(2,1)}), bf16[8,128,768]{2,1,0:T(8,128)(2,1)S(1)}, u32[]{:S(2)}, u32[]{:S(2)}) async-start(bf16[8,128,768]{2,1,0:T(8,128)(2,1)} %bitcast.165), calls=%async_computation.1 | async-start | bytes 3145728 | tf_op jit(solution)/shard_map/all_to_all | solution.py:391
  160.5 120.6 %copy-start.20 = (f32[512,8]{0,1:T(8,128)}, f32[512,8]{0,1:T(8,128)S(1)}, u32[]{:S(2)}) copy-start(f32[512,8]{0,1:T(8,128)S(1)} %get-tuple-element.286) | copy-start | bytes 49156
  160.5 120.6 %copy-start.38 = (f32[512]{0:T(512)}, f32[512]{0:T(512)S(1)}, u32[]{:S(2)}) copy-start(f32[512]{0:T(512)S(1)} %get-tuple-element.285) | copy-start | bytes 6148
  160.5 120.5 %copy-start.42 = (f32[512]{0:T(512)}, f32[512]{0:T(512)S(1)}, u32[]{:S(2)}) copy-start(f32[512]{0:T(512)S(1)} %fusion.92) | copy-start | bytes 6148
  160.5 120.5 %copy-start.52 = (f32[8]{0:T(128)}, f32[8]{0:T(128)S(1)}, u32[]{:S(2)}) copy-start(f32[8]{0:T(128)S(1)} %broadcast_multiply_fusion.6) | copy-start | bytes 100
  199.9 81.2 %copy-start.40 = (f32[512]{0:T(512)}, f32[512]{0:T(512)S(1)}, u32[]{:S(2)}) copy-start(f32[512]{0:T(512)S(1)} %fusion.67) | copy-start | bytes 6148
  200.6 80.5 %copy-start.45 = (f32[512]{0:T(512)}, f32[512]{0:T(512)S(1)}, u32[]{:S(2)}) copy-start(f32[512]{0:T(512)S(1)} %get-tuple-element.237) | copy-start | bytes 6148
  203.6 10.0 %all-to-all-start.2 = ((f32[8,1,128]{2,1,0:T(1,128)}), f32[8,1,128]{2,1,0:T(1,128)S(1)}, u32[]{:S(2)}, u32[]{:S(2)}) async-start(f32[8,1,128]{2,1,0:T(1,128)} %bitcast.18), calls=%async_computation.2 | async-start | bytes 8192 | tf_op jit(solution)/shard_map/all_to_all | solution.py:404
  207.2 110.2 %all-gather.2.cloned.1.call-start = ((), (), s32[]{:S(2)}) async-start(), calls=%async_computation.11 | async-start | bytes 3932160 | tf_op jit(solution)/shard_map/all_gather | solution.py:470
  289.5 301.5 %reduce-scatter.30.cloned.1.call-start = ((), (), s32[]{:S(2)}) async-start(), calls=%async_computation.18 | async-start | bytes 245760
  302.3 290.2 %reduce-scatter.28.cloned.1.call-start = ((), (), s32[]{:S(2)}) async-start(), calls=%async_computation.17 | async-start | bytes 983040
  305.2 311.1 %reduce-scatter.26.cloned.1.call-start = ((), (), s32[]{:S(2)}) async-start(), calls=%async_computation.16 | async-start | bytes 442368
  543.6 128.1 %reduce-scatter.24.cloned.1.call-start = ((), (), s32[]{:S(2)}) async-start(), calls=%async_computation.15 | async-start | bytes 1105920
  558.6 162.3 %reduce-scatter.22.cloned.1.call-start = ((), (), s32[]{:S(2)}) async-start(), calls=%async_computation.14 | async-start | bytes 5898240 | tf_op jit(solution)/shard_map/reduce_scatter | solution.py:439
  567.8 203.7 %reduce-scatter.20.cloned.1.call-start = ((), (), s32[]{:S(2)}) async-start(), calls=%async_computation.13 | async-start | bytes 5898240 | tf_op jit(solution)/shard_map/reduce_scatter | solution.py:436
  578.8 233.2 %reduce-scatter.18.cloned.1.call-start = ((), (), s32[]{:S(2)}) async-start(), calls=%async_computation.12 | async-start | bytes 3932160 | tf_op jit(solution)/shard_map/reduce_scatter | solution.py:527
  673.7 138.3 %copy-start.37 = (f32[768]{0:T(1024)S(1)}, f32[768]{0:T(1024)}, u32[]{:S(2)}) copy-start(f32[768]{0:T(1024)} %g1_ref.1) | copy-start | bytes 9220
  723.8 90.2 %copy-start.44 = (f32[768]{0:T(1024)S(1)}, f32[768]{0:T(1024)}, u32[]{:S(2)}) copy-start(f32[768]{0:T(1024)} %get-tuple-element.270) | copy-start | bytes 9220
  723.8 90.2 %copy-start.49 = (f32[768]{0:T(1024)S(1)}, f32[768]{0:T(1024)}, u32[]{:S(2)}) copy-start(f32[768]{0:T(1024)} %get-tuple-element.229) | copy-start | bytes 9220
  723.8 90.2 %copy-start.50 = (f32[768]{0:T(1024)S(1)}, f32[768]{0:T(1024)}, u32[]{:S(2)}) copy-start(f32[768]{0:T(1024)} %get-tuple-element.234) | copy-start | bytes 9220
  723.8 133.9 %copy-start.9 = (f32[512,768]{1,0:T(8,128)S(1)}, f32[512,768]{1,0:T(8,128)}, u32[]{:S(2)}) copy-start(f32[512,768]{1,0:T(8,128)} %copy-done.8) | copy-start | bytes 4718596
  771.5 89.0 %copy-start.1 = (f32[768,8]{0,1:T(8,128)S(1)}, f32[768,8]{0,1:T(8,128)}, u32[]{:S(2)}) copy-start(f32[768,8]{0,1:T(8,128)} %param.28) | copy-start | bytes 73732
  (54 other events, 393.2 us)
Sparse Core Ops, SparseCore 0:
  289.7 27.7 all-gather.1
  320.5 19.7 reduce-scatter.29
  342.8 23.2 reduce-scatter.27
  543.7 61.3 reduce-scatter.25
  609.2 62.3 reduce-scatter.23
  674.0 46.8 reduce-scatter.21
  723.6 47.8 reduce-scatter.19
  774.0 37.9 reduce-scatter.17

commit v2 on v1

v2 whole, which is shorter than its diff:
```python
import functools
import jax
import jax.numpy as jnp
from jax import lax
from jax.experimental import pallas as pl
from jax.experimental.pallas import tpu as pltpu
from jax.sharding import PartitionSpec as P

EPSILON = 1e-05
BAL_COEF = 0.01
HIGHEST = lax.Precision.HIGHEST
NEG_LARGE = -1e30
MESH = pl.DeviceIdType.MESH
F32 = jnp.float32
BF16 = jnp.bfloat16
TILE = 256
VMEM_LIMIT = 60 << 20


def flip(index, bits):
    out, bit = index, 1
    while bit <= bits:
        if bits & bit:
            out = out + bit - 2 * bit * lax.rem(lax.div(index, bit), 2)
        bit *= 2
    return out


def remote(src, dst, send_sem, recv_sem, device):
    return pltpu.make_async_remote_copy(
        src_ref=src, dst_ref=dst, send_sem=send_sem, recv_sem=recv_sem, device_id=device, device_id_type=MESH
    )


def dot(left, right, dims=((1,), (0,)), precision=None):
    return lax.dot_general(left, right, (dims, ((), ())), precision=precision, preferred_element_type=F32)


def normalize(values, gain, bias):
    average = jnp.mean(values, axis=-1, keepdims=True)
    centred = values - average
    variance = jnp.mean(centred * centred, axis=-1, keepdims=True)
    inverse = lax.rsqrt(variance + EPSILON)
    scaled = centred * inverse
    return (scaled * gain + bias, scaled, inverse)


def norm_backward(grad_normed, scaled, inverse, gain):
    grad_scaled = grad_normed * gain
    first_mean = jnp.mean(grad_scaled, axis=-1, keepdims=True)
    second_mean = jnp.mean(grad_scaled * scaled, axis=-1, keepdims=True)
    return inverse * (grad_scaled - first_mean - scaled * second_mean)


def slot_layouts(routes, experts, cap):
    rows = routes.shape[1]
    count = max(8, experts)
    expert = lax.broadcasted_iota(jnp.int32, (count, rows), 0)
    hot = (routes == expert).astype(F32)
    upto = lax.broadcasted_iota(jnp.int32, (rows, rows), 0) <= lax.broadcasted_iota(jnp.int32, (rows, rows), 1)
    rank = dot(hot.astype(BF16), upto.astype(F32).astype(BF16))
    slot_row = jnp.sum((rank - 1.0) * hot, axis=0, keepdims=True)
    flat_row = jnp.sum((rank - 1.0 + cap * expert.astype(F32)) * hot, axis=0, keepdims=True)
    return hot, flat_row.astype(jnp.int32), slot_row.astype(jnp.int32)


def barrier_signal(peers):
    barrier = pltpu.get_barrier_semaphore()
    for peer in peers:
        pl.semaphore_signal(barrier, inc=1, device_id=peer, device_id_type=MESH)


def barrier_wait(count):
    pl.semaphore_wait(pltpu.get_barrier_semaphore(), count)


def kernel_a(
    n_dp, x_ref, g1_ref, b1_ref, w_ref, qb_ref, proj_ref, routes_ref, cot_ref, len_ref,
    gath_o, qkv_o, p_o, ctx_o, ctxf_o, projf_o, cots_o,
    gath, qkv, p_st, bias_s, ctx_s, disp,
    ag_s, ag_r, pj_s, pj_r, cx_s, cx_r, ct_s, ct_r, p_sem, loc,
):
    tok, width = x_ref.shape
    heads = qb_ref.shape[0]
    hd = qb_ref.shape[2]
    group = 4 * tok
    tiles = group // TILE
    reach = group // 2 // TILE + 1
    cap = cots_o.shape[0] // n_dp
    d = lax.axis_index("dp")
    h = lax.axis_index("head")
    barrier_signal([(d, flip(h, k)) for k in (1, 2, 3)] + [(flip(d, r), h) for r in range(1, n_dp)])

    normed, _, _ = normalize(x_ref[...].astype(F32), g1_ref[...][None, :], b1_ref[...][None, :])

    def block(index):
        return pl.ds(pl.multiple_of(index * tok, tok), tok)

    gath[block(h), :] = normed.astype(BF16)
    barrier_wait(3 + n_dp - 1)

    chunks = 4
    step = tok // chunks

    def part(index, i):
        return gath.at[pl.ds(pl.multiple_of(index * tok + i * step, step), step), :]

    sib, cross, diag = flip(h, 1), flip(h, 2), flip(h, 3)
    to_cross = [remote(part(h, i), part(h, i), ag_s.at[i], ag_r.at[i], (d, cross)) for i in range(chunks)]
    to_sib = remote(gath.at[block(h), :], gath.at[block(h), :], ag_s.at[2 * chunks], ag_r.at[2 * chunks], (d, sib))
    onward = [
        remote(part(cross, i), part(cross, i), ag_s.at[chunks + i], ag_r.at[chunks + i], (d, sib)) for i in range(chunks)
    ]
    for copy in to_cross:
        copy.start()
    to_sib.start()
    proj_copies = [
        remote(proj_ref, projf_o.at[h], pj_s.at[k], pj_r.at[k], (d, flip(h, k))) for k in (1, 2, 3)
    ]

    hot_t, flat_row, slot_row = slot_layouts(routes_ref[...], n_dp, cap)
    slot_iota = lax.broadcasted_iota(jnp.int32, (cap, tok), 0)

    def dispatch(e, carry):
        hot = (flat_row == slot_iota + e * cap).astype(F32).astype(BF16)
        disp[pl.ds(pl.multiple_of(e * cap, cap), cap), :] = dot(hot, cot_ref[...]).astype(BF16)
        return carry

    lax.fori_loop(0, n_dp, dispatch, 0)

    def slots(index):
        return pl.ds(pl.multiple_of(index * cap, cap), cap)

    cot_copies = [
        remote(disp.at[slots(flip(d, r)), :], cots_o.at[pl.ds(r * cap, cap), :], ct_s.at[r], ct_r.at[r], (flip(d, r), h))
        for r in range(1, n_dp)
    ]
    for copy in cot_copies:
        copy.start()
    cot_own = pltpu.make_async_copy(disp.at[slots(d), :], cots_o.at[pl.ds(0, cap), :], ct_s.at[0])
    cot_own.start()

    def project(index):
        rows = gath[block(index), :]
        for c in range(3):
            out = dot(rows, w_ref[c], ((1,), (1,)))
            for a in range(heads):
                piece = out[:, a * hd : (a + 1) * hd]
                if c != 1:
                    piece = piece + qb_ref[a, c // 2 : c // 2 + 1, :]
                piece = piece.astype(BF16)
                if c == 0:
                    piece = piece * jnp.asarray(hd ** (-0.5), BF16)
                qkv[c, a, block(index), :] = piece

    project(h)
    to_sib.wait_recv()
    project(sib)
    for i in range(chunks):
        to_cross[i].wait_recv()
        onward[i].start()
    for copy in proj_copies:
        copy.start()
    proj_own = pltpu.make_async_copy(proj_ref, projf_o.at[h], loc.at[0])
    proj_own.start()
    project(cross)
    for i in range(chunks):
        onward[i].wait_recv()
    project(diag)
    gath_copy = pltpu.make_async_copy(gath, gath_o, loc.at[1])
    gath_copy.start()
    qkv_copy = pltpu.make_async_copy(qkv, qkv_o, loc.at[2])
    qkv_copy.start()

    ends = [len_ref[0, 0]]
    for i in range(1, len_ref.shape[1] - 1):
        ends.append(ends[-1] + len_ref[0, i])

    order = []
    for i in range(tiles // 2):
        order += [tiles - 1 - i, tiles // 2 - 1 - i]
    per_block = tok // TILE

    def p_copy(t, a):
        size = min(t + 1, reach) * TILE
        return pltpu.make_async_copy(p_st.at[a, :, pl.ds(0, size)], p_o.at[a, t, :, pl.ds(0, size)], p_sem.at[a])

    previous = None
    for t in order:
        size = min(t + 1, reach) * TILE
        first = (t + 1) * TILE - size
        row = t * TILE + lax.broadcasted_iota(jnp.int32, (TILE, 1), 0)
        start = jnp.zeros((TILE, 1), jnp.int32)
        for end in ends:
            start = jnp.where(row >= end, end, start)
        col = first + lax.broadcasted_iota(jnp.int32, (TILE, size), 1)
        bias_s[:, :size] = jnp.where((col >= start) & (col <= row), 0.0, NEG_LARGE)
        outs = []
        for a in range(heads):
            q = qkv[0, a, t * TILE : (t + 1) * TILE, :]
            k = qkv[1, a, first : (t + 1) * TILE, :]
            v = qkv[2, a, first : (t + 1) * TILE, :]
            s = dot(q, k, ((1,), (1,))) + bias_s[:, :size]
            top = jnp.max(s, axis=1, keepdims=True)
            e = jnp.exp(s - top)
            total = jnp.sum(e, axis=1, keepdims=True)
            p = (e * (1.0 / total)).astype(BF16)
            if previous is not None:
                p_copy(previous, a).wait()
            p_st[a, :, :size] = p
            p_copy(t, a).start()
            outs.append(dot(p, v))
        ctx_s[t] = jnp.concatenate(outs, axis=1).astype(BF16)
        previous = t
        owner, sub = t // per_block, t % per_block
        rows = pl.ds(sub * TILE, TILE)

        @pl.when(h != owner)
        def _():
            remote(ctx_s.at[t], ctxf_o.at[h, rows, :], cx_s.at[t], cx_r.at[h, sub], (d, owner)).start()

        @pl.when(h == owner)
        def _():
            pltpu.make_async_copy(ctx_s.at[t], ctxf_o.at[h, rows, :], cx_s.at[t]).start()

    ctx_copy = pltpu.make_async_copy(ctx_s, ctx_o, loc.at[3])
    ctx_copy.start()
    for a in range(heads):
        p_copy(previous, a).wait()
    for t in range(tiles):
        owner, sub = t // per_block, t % per_block
        rows = pl.ds(sub * TILE, TILE)

        @pl.when(h != owner)
        def _():
            remote(ctx_s.at[t], ctxf_o.at[h, rows, :], cx_s.at[t], cx_r.at[h, sub], (d, owner)).wait_send()

        @pl.when(h == owner)
        def _():
            pltpu.make_async_copy(ctx_s.at[t], ctxf_o.at[h, rows, :], cx_s.at[t]).wait()

    for k in (1, 2, 3):
        peer = flip(h, k)
        for sub in range(per_block):
            remote(
                ctx_s.at[0], ctxf_o.at[peer, pl.ds(sub * TILE, TILE), :], cx_s.at[0], cx_r.at[peer, sub], (d, peer)
            ).wait_recv()
    for copy in to_cross:
        copy.wait_send()
    to_sib.wait_send()
    for copy in onward:
        copy.wait_send()
    for k in (1, 2, 3):
        proj_copies[k - 1].wait_send()
        peer = flip(h, k)
        remote(proj_ref, projf_o.at[peer], pj_s.at[k], pj_r.at[k], (d, peer)).wait_recv()
    for copy in cot_copies:
        copy.wait()
    for copy in (cot_own, proj_own, gath_copy, qkv_copy, ctx_copy):
        copy.wait()


VM = pl.BlockSpec(memory_space=pltpu.VMEM)
SM = pl.BlockSpec(memory_space=pltpu.SMEM)
ANY = pl.BlockSpec(memory_space=pl.ANY)
DMA = pltpu.SemaphoreType.DMA


def stage_a(n_dp, x, g1, b1, w, qb, proj, routes, cot, lengths, cap):
    tok, width = x.shape
    heads, hd = qb.shape[1:]
    w, qb, routes = w.transpose(0, 2, 1), qb.transpose(1, 0, 2), routes.T
    group = 4 * tok
    tiles = group // TILE
    span = (group // 2 // TILE + 1) * TILE
    cols = heads * hd
    sds = jax.ShapeDtypeStruct
    return pl.pallas_call(
        functools.partial(kernel_a, n_dp),
        out_shape=(
            sds((group, width), BF16),
            sds((3, heads, group, hd), BF16),
            sds((heads, tiles, TILE, span), BF16),
            sds((tiles, TILE, cols), BF16),
            sds((4, tok, cols), BF16),
            sds((4, cols, width), BF16),
            sds((n_dp * cap, width), BF16),
        ),
        in_specs=[VM] * 8 + [SM],
        out_specs=(ANY,) * 7,
        scratch_shapes=[
            pltpu.VMEM((group, width), BF16),
            pltpu.VMEM((3, heads, group, hd), BF16),
            pltpu.VMEM((heads, TILE, span), BF16),
            pltpu.VMEM((TILE, span), F32),
            pltpu.VMEM((tiles, TILE, cols), BF16),
            pltpu.VMEM((n_dp * cap, width), BF16),
            DMA((9,)), DMA((9,)), DMA((4,)), DMA((4,)), DMA((tiles,)), DMA((4, tok // TILE)),
            DMA((n_dp,)), DMA((n_dp,)), DMA((heads,)), DMA((4,)),
        ],
        compiler_params=pltpu.CompilerParams(collective_id=0, has_side_effects=True, vmem_limit_bytes=VMEM_LIMIT),
    )(x, g1, b1, w, qb, proj, routes, cot, lengths)


def far_first(n_dp):
    half = n_dp // 2
    return list(range(half, n_dp)) + [r for r in range(2, half)] + [1]


def gelu_parts(u):
    density = jnp.exp(u * u * -0.5)
    t = 1.0 / (1.0 + jnp.abs(u) * (0.3275911 * 0.7071067811865476))
    poly = ((((1.061405429 * t - 1.453152027) * t + 1.421413741) * t - 0.284496736) * t + 0.254829592) * t
    tail = 0.5 * poly * density
    return jnp.where(u < 0.0, tail, 1.0 - tail), density * 0.3989422804014327


def row_to_col(row):
    return jnp.broadcast_to(row, (128, row.shape[1])).T[:, :1]


def col_to_rows(col):
    return jnp.broadcast_to(col, (col.shape[0], 128)).T[:8]


def kernel_m(
    n_dp, x_ref, ctxf, projf, pb_ref, g2_ref, b2_ref, rt_ref, routes_ref, cot_ref, cots, up_h, upb_ref, down_h, downb_ref,
    res_o, gate_o, prod_o, gres_o, gctx_o, upc_o, upo_o, dng_o, sm_o, bg_o, bal_o,
    res, stat, disp, gsend, rows, grecv, up, down, ghu, hid, gg, gacc, gin, ggs, ginr, ggr, dsend, dacc, drecv, urecv,
    ld, ra_s, ra_r, ga_s, ga_r, rb_s, rb_r, gb_s, gb_r, ds_s, ds_r, us_s, us_r, out_sem,
):
    tok, width = x_ref.shape
    ff = up.shape[1]
    slots = rows.shape[0]
    cap = slots // n_dp
    per = TILE // cap
    groups = slots // TILE
    experts = n_dp
    quarter = ff // 4
    d = lax.axis_index("dp")
    h = lax.axis_index("head")
    sib, cross = (d, flip(h, 1)), (d, flip(h, 2))
    loads = [pltpu.make_async_copy(down_h.at[0], down, ld.at[0]), pltpu.make_async_copy(up_h.at[0], up, ld.at[1])]
    for copy in loads:
        copy.start()
    barrier_signal([(d, flip(h, k)) for k in (1, 2, 3)] + [(flip(d, r), h) for r in range(1, n_dp)])

    attended = dot(ctxf[0], projf[0])
    for b in range(1, 4):
        attended += dot(ctxf[b], projf[b])
    residual = x_ref[...].astype(F32) + attended + pb_ref[...][None, :]
    res[...] = residual
    average = jnp.mean(residual, axis=-1, keepdims=True)
    centred = residual - average
    inverse = lax.rsqrt(jnp.mean(centred * centred, axis=-1, keepdims=True) + EPSILON)
    stat[0] = average
    stat[1] = inverse
    gain, bias = g2_ref[...][None, :], b2_ref[...][None, :]
    normed = centred * inverse * gain + bias
    logits = dot(rt_ref[...], normed, ((1,), (1,)), HIGHEST)
    raised = jnp.exp(logits - jnp.max(logits, axis=0, keepdims=True))
    prob = raised / jnp.sum(raised, axis=0, keepdims=True)
    hot, flat_row, slot_row = slot_layouts(routes_ref[...], experts, cap)
    hot = hot[:experts]
    gate_row = jnp.sum(prob * hot, axis=0, keepdims=True)
    gate_o[...] = row_to_col(gate_row)
    fraction = jnp.mean(hot, axis=1, keepdims=True)
    bal_o[...] = experts * jnp.sum(fraction * jnp.mean(prob, axis=1, keepdims=True), axis=0, keepdims=True)

    expert_row = jnp.sum(hot * lax.broadcasted_iota(jnp.int32, hot.shape, 0).astype(F32), axis=0, keepdims=True)
    other_row = jnp.bitwise_xor(expert_row.astype(jnp.int32), d)
    flat_x = other_row * cap + slot_row
    at_slot = (slot_row == lax.broadcasted_iota(jnp.int32, (128, tok), 0)).astype(F32)
    other_hot = (other_row == lax.broadcasted_iota(jnp.int32, (max(8, n_dp), tok), 0)).astype(F32)
    gates = dot(other_hot * gate_row, at_slot, ((1,), (1,)), HIGHEST)
    normed_low = normed.astype(BF16)
    barrier_wait(3 + n_dp - 1)
    order = far_first(n_dp)

    def send_rows(r):
        return remote(disp.at[pl.ds(r * cap, cap), :], rows.at[pl.ds(r * cap, cap), :], ra_s.at[r], ra_r.at[r], (flip(d, r), h))

    def send_gate(r):
        return remote(gsend.at[r], grecv.at[r], ga_s.at[r], ga_r.at[r], (flip(d, r), h))

    slot_iota = lax.broadcasted_iota(jnp.int32, (cap, tok), 0)
    for r in order + [0]:
        hits = (flat_x == slot_iota + r * cap).astype(F32).astype(BF16)
        block = dot(hits, normed_low).astype(BF16)
        gsend[r] = jnp.broadcast_to(gates[r : r + 1], (8, 128))
        if r:
            disp[r * cap : (r + 1) * cap, :] = block
            send_rows(r).start()
            send_gate(r).start()
        else:
            rows[:cap, :] = block
            grecv[0] = gsend[0]

    loads[0].wait()

    def hidden_grad(i, carry):
        at = pl.ds(pl.multiple_of(lax.div(i, 4) * TILE, TILE), TILE)
        cols = pl.ds(pl.multiple_of(lax.rem(i, 4) * quarter, quarter), quarter)
        ghu[at, cols] = dot(cots[at, :], down[cols, :], ((1,), (1,))).astype(BF16)
        return carry

    lax.fori_loop(0, 4 * groups, hidden_grad, 0)
    loads[1].wait()

    step = 512

    def send_back(r):
        return remote(gin.at[pl.ds(r * cap, cap), :], ginr.at[pl.ds(r * cap, cap), :], rb_s.at[r], rb_r.at[r], (flip(d, r), h))

    def send_gg(r):
        return remote(ggs.at[r // per], ggr.at[r], gb_s.at[r], gb_r.at[r], (flip(d, r), h))

    for g in range(groups):
        mine = [r for r in range(g * per, (g + 1) * per)]
        for r in mine:
            if r:
                send_rows(r).wait_recv()
                send_gate(r).wait_recv()
        at = slice(g * TILE, (g + 1) * TILE)
        gate = jnp.concatenate([grecv[r].T[:cap, :1] for r in mine], axis=0)
        gacc[...] = jnp.zeros_like(gacc)
        gg[...] = jnp.zeros_like(gg)

        def expert(f, carry):
            cols = pl.ds(pl.multiple_of(f * step, step), step)
            u = dot(rows[at, :], up[:, cols]) + upb_ref[:, cols]
            share, density = gelu_parts(u)
            out = u * share
            low = out.astype(BF16)
            back = ghu[at, cols].astype(F32)
            hid[at, cols] = low
            meet = low.astype(F32) * back
            folded = meet[:, :128]
            for j in range(1, step // 128):
                folded += meet[:, j * 128 : (j + 1) * 128]
            gg[...] += folded
            pre = (gate * back * (share + u * density)).astype(BF16)
            ghu[at, cols] = pre
            gacc[...] += dot(pre, up[:, cols], ((1,), (1,)))
            return carry

        lax.fori_loop(0, ff // step, expert, 0)
        cot_g = cots[at, :].astype(F32)
        gg_col = jnp.sum(gg[...], axis=1, keepdims=True) + jnp.sum(cot_g * downb_ref[...], axis=1, keepdims=True)
        ggs[g] = col_to_rows(gg_col)
        if g == 0:
            gin[at, :] = gacc[...].astype(BF16)
            ginr[:cap, :] = gin[:cap, :]
            ggr[0] = ggs[0]
        else:
            gin[at, :] = gacc[...].astype(BF16)
        for r in mine:
            if r:
                send_back(r).start()
                send_gg(r).start()
        cots[at, :] = (gate * cot_g).astype(BF16)

    third = quarter // 3

    def block_cols(index):
        return pl.ds(pl.multiple_of(index * quarter, quarter), quarter)

    def down_block(index, put):
        def body(i, carry):
            cols = pl.ds(pl.multiple_of(index * quarter + i * third, third), third)
            put(pl.ds(pl.multiple_of(i * third, third), third), dot(hid[:, cols], cots[...], ((0,), (0,))))
            return carry

        lax.fori_loop(0, 3, body, 0)

    def up_block(index, put):
        part = width // 3

        def body(i, carry):
            cols = pl.ds(pl.multiple_of(i * part, part), part)
            put(cols, dot(rows[:, cols], ghu[:, block_cols(index)], ((0,), (0,))))
            return carry

        lax.fori_loop(0, 3, body, 0)

    def store(ref, kind):
        def put(at, value):
            ref[at, :] = value.astype(kind)

        return put

    down_sib = [remote(dsend.at[i], drecv.at[i], ds_s.at[i], ds_r.at[i], sib) for i in range(2)]
    down_cross = remote(dacc, drecv.at[2], ds_s.at[2], ds_r.at[2], cross)
    up_sib = [remote(dsend.at[i], urecv.at[i], us_s.at[i], us_r.at[i], sib) for i in range(2)]
    down_block(flip(h, 3), store(dsend.at[1], BF16))
    down_sib[1].start()
    down_block(flip(h, 1), store(dsend.at[0], BF16))
    down_sib[0].start()
    down_block(flip(h, 2), store(dacc, BF16))
    down_sib[1].wait_recv()
    dacc[...] = (dacc[...].astype(F32) + drecv[1].astype(F32)).astype(BF16)
    down_cross.start()
    for r in order:
        send_rows(r).wait_send()

    def produce(i, carry):
        at = pl.ds(pl.multiple_of(i * TILE, TILE), TILE)
        disp[at, :] = (dot(hid[at, :], down[...]) + downb_ref[...]).astype(BF16)
        return carry

    lax.fori_loop(0, groups, produce, 0)
    prod_copy = pltpu.make_async_copy(disp, prod_o, out_sem.at[0])
    prod_copy.start()
    res_copy = pltpu.make_async_copy(res, res_o, out_sem.at[1])
    res_copy.start()
    for copy in down_sib:
        copy.wait_send()
    up_block(flip(h, 3), store(dsend.at[1], BF16))
    up_sib[1].start()
    up_block(flip(h, 1), store(dsend.at[0], BF16))
    up_sib[0].start()
    up_block(flip(h, 2), store(upc_o, BF16))
    up_block(h, store(upo_o, F32))
    down_block(h, store(dng_o, F32))
    ones = jnp.ones((8, slots), BF16)
    up_bias = dot(ones, ghu[...])
    down_bias = dot(ones, cots[...])
    short = width // 4
    for b in range(4):
        bg_o[b, 0:1, :] = up_bias[:1, b * quarter : (b + 1) * quarter]
        bg_o[b, 1:2, :short] = down_bias[:1, b * short : (b + 1) * short]
    up_sib[1].wait_recv()
    upc_o[...] = (upc_o[...].astype(F32) + urecv[1].astype(F32)).astype(BF16)
    up_sib[0].wait_recv()
    upo_o[...] = upo_o[...] + urecv[0].astype(F32)
    down_sib[0].wait_recv()
    dng_o[...] = dng_o[...] + drecv[0].astype(F32)

    flat_col = row_to_col(flat_x.astype(F32)).astype(jnp.int32)
    pick = (flat_col == lax.broadcasted_iota(jnp.int32, (tok, slots), 1)).astype(F32).astype(BF16)
    for r in order:
        send_back(r).wait_recv()
        send_gg(r).wait_recv()
    gin_tok = dot(pick, ginr[...])
    slot_gg = [ggr[r][:1, (r % per) * cap : (r % per) * cap + cap] for r in range(n_dp)]
    slot_gg = jnp.concatenate(slot_gg + [jnp.zeros_like(slot_gg[0])] * (max(8, n_dp) - n_dp), axis=0)
    grad_gate = jnp.sum(dot(slot_gg, at_slot[:cap], precision=HIGHEST) * other_hot, axis=0, keepdims=True)
    grad_prob = hot * grad_gate + (BAL_COEF * experts / tok) * fraction
    grad_logits = prob * (grad_prob - jnp.sum(prob * grad_prob, axis=0, keepdims=True))
    average, inverse = stat[0], stat[1]
    scaled = (res[...] - average) * inverse
    normed = scaled * gain + bias
    padded = jnp.concatenate([grad_logits, jnp.zeros((128 - experts, tok), F32)], axis=0)
    logits_col = padded.T[:, :experts]
    grad_normed = gin_tok + dot(logits_col, rt_ref[...], precision=HIGHEST)
    grad_res = cot_ref[...].astype(F32) + norm_backward(grad_normed, scaled, inverse, gain)
    gres_o[...] = grad_res
    sm_o[...] = jnp.zeros_like(sm_o)
    sm_o[0:1, :] = jnp.sum(grad_normed * scaled, axis=0, keepdims=True)
    sm_o[1:2, :] = jnp.sum(grad_normed, axis=0, keepdims=True)
    sm_o[2:3, :] = jnp.sum(grad_res, axis=0, keepdims=True)
    sm_o[8 : 8 + experts, :] = dot(grad_logits, normed, precision=HIGHEST)
    low = grad_res.astype(BF16)
    for b in range(4):
        gctx_o[b] = dot(low, projf[b], ((1,), (1,))).astype(BF16)

    down_cross.wait_recv()
    dng_o[...] = dng_o[...] + drecv[2].astype(F32)
    down_cross.wait_send()
    for copy in up_sib:
        copy.wait_send()
    for r in order:
        send_gate(r).wait_send()
        send_back(r).wait_send()
        send_gg(r).wait_send()
    prod_copy.wait()
    res_copy.wait()


def stage_m(n_dp, x, ctxf, projf, pb, g2, b2, router, routes, cot, cots, up, upb, down, downb):
    tok, width = x.shape
    slots = cots.shape[0]
    ff = up.shape[2]
    cols = ctxf.shape[2]
    cap = slots // n_dp
    groups = slots // TILE
    quarter = ff // 4
    sds = jax.ShapeDtypeStruct
    return pl.pallas_call(
        functools.partial(kernel_m, n_dp),
        out_shape=(
            sds((tok, width), F32),
            sds((tok, 1), F32),
            sds((slots, width), BF16),
            sds((tok, width), F32),
            sds((4, tok, cols), BF16),
            sds((width, quarter), BF16),
            sds((width, quarter), F32),
            sds((quarter, width), F32),
            sds((8 + max(8, n_dp), width), F32),
            sds((4, 8, quarter), F32),
            sds((1, 1), F32),
        ),
        in_specs=[VM] * 10 + [ANY, VM, ANY, VM],
        out_specs=(ANY, VM, ANY) + (VM,) * 8,
        scratch_shapes=[
            pltpu.VMEM((tok, width), F32),
            pltpu.VMEM((2, tok, 1), F32),
            pltpu.VMEM((slots, width), BF16),
            pltpu.VMEM((n_dp, 8, 128), F32),
            pltpu.VMEM((slots, width), BF16),
            pltpu.VMEM((n_dp, 8, 128), F32),
            pltpu.VMEM((width, ff), BF16),
            pltpu.VMEM((ff, width), BF16),
            pltpu.VMEM((slots, ff), BF16),
            pltpu.VMEM((slots, ff), BF16),
            pltpu.VMEM((TILE, 128), F32),
            pltpu.VMEM((TILE, width), F32),
            pltpu.VMEM((slots, width), BF16),
            pltpu.VMEM((groups, 8, TILE), F32),
            pltpu.VMEM((slots, width), BF16),
            pltpu.VMEM((n_dp, 8, TILE), F32),
            pltpu.VMEM((2, quarter, width), BF16),
            pltpu.VMEM((quarter, width), BF16),
            pltpu.VMEM((3, quarter, width), BF16),
            pltpu.VMEM((2, width, quarter), BF16),
            DMA((2,)), DMA((n_dp,)), DMA((n_dp,)), DMA((n_dp,)), DMA((n_dp,)), DMA((n_dp,)), DMA((n_dp,)),
            DMA((n_dp,)), DMA((n_dp,)), DMA((3,)), DMA((3,)), DMA((2,)), DMA((2,)), DMA((2,)),
        ],
        compiler_params=pltpu.CompilerParams(collective_id=1, has_side_effects=True, vmem_limit_bytes=VMEM_LIMIT),
    )(x, ctxf, projf, pb, g2, b2, router.T, routes.T, cot, cots, up, upb, down, downb)


def kernel_b(
    n_dp, gctx, qkv_h, p_h, ctx, ctxf, gath_h, w_ref, x_ref, g1_ref, b1_ref, gres, prod_h, upc_h, sm_ref, bg_ref,
    igrad_o, prodr_o, upr_o, qg_o, pg_o, qb_o, sums_o, ends_o, bgs_o,
    gcr, qkv, p_v, gath, dk, dv, grads, gsend, gacc, grecv, qg, qgr, pg, pgr, pacc, qb, qbr, smr, smd, smt, en, enr, ent, enq, bgr,
    ld, p_sem, gc_s, gc_r, pr_s, pr_r, uc_s, uc_r, gn_s, gn_r, qg_s, qg_r, pg_s, pg_r, pt_s, pt_r, qb_s, qb_r,
    sh_s, sh_r, sd_s, sd_r, eh_s, eh_r, ed_s, ed_r, bg_s, bg_r,
):
    tok, width = x_ref.shape
    heads, group, hd = qkv.shape[1:]
    cols = heads * hd
    tiles = group // TILE
    reach = group // 2 // TILE + 1
    per_block = tok // TILE
    slots = prod_h.shape[0]
    cap = slots // n_dp
    share = width // n_dp
    d = lax.axis_index("dp")
    h = lax.axis_index("head")
    sib, cross = (d, flip(h, 1)), (d, flip(h, 2))
    order = far_first(n_dp)

    def at_head(k):
        return (d, flip(h, k))

    def at_dp(r):
        return (flip(d, r), h)

    def p_load(t, slot):
        size = min(t + 1, reach) * TILE
        return pltpu.make_async_copy(p_h.at[:, t, :, pl.ds(0, size)], p_v.at[slot, :, :, pl.ds(0, size)], p_sem.at[slot])

    load_qkv = pltpu.make_async_copy(qkv_h, qkv, ld.at[0])
    load_qkv.start()
    barrier_signal([at_head(k) for k in (1, 2, 3)] + [at_dp(r) for r in range(1, n_dp)])
    load_gath = pltpu.make_async_copy(gath_h, gath, ld.at[1])
    dk[...] = jnp.zeros_like(dk)
    dv[...] = jnp.zeros_like(dv)
    barrier_wait(3 + n_dp - 1)

    def send_ctx(k):
        return remote(gctx.at[flip(h, k)], gcr.at[h], gc_s.at[k], gc_r.at[k], at_head(k))

    for k in (2, 3, 1):
        send_ctx(k).start()

    def send_prod(r):
        rows = pl.ds(r * cap, cap)
        return remote(prod_h.at[rows, :], prodr_o.at[rows, :], pr_s.at[r], pr_r.at[r], at_dp(r))

    for r in order:
        send_prod(r).start()
    prod_own = pltpu.make_async_copy(prod_h.at[pl.ds(0, cap), :], prodr_o.at[pl.ds(0, cap), :], pr_s.at[0])
    prod_own.start()
    gcr[h] = gctx[h]

    sm_head = [remote(sm_ref, smr.at[k], sh_s.at[k], sh_r.at[k], at_head(k)) for k in (1, 2, 3)]
    for copy in sm_head:
        copy.start()
    bg_head = [remote(bg_ref.at[flip(h, k)], bgr.at[k], bg_s.at[k], bg_r.at[k], at_head(k)) for k in (1, 2, 3)]
    for copy in bg_head:
        copy.start()

    low = gres[...].astype(BF16)

    def proj_block(index):
        return dot(low, ctxf[index], ((0,), (0,))).astype(BF16)

    pg[1] = proj_block(flip(h, 3))
    pg[0] = proj_block(flip(h, 1))
    pg_sib = [remote(pg.at[i], pgr.at[i], pg_s.at[i], pg_r.at[i], sib) for i in range(2)]
    for copy in pg_sib:
        copy.start()
    pg[2] = proj_block(flip(h, 2))
    pacc[...] = dot(low, ctxf[h], ((0,), (0,)))
    pg_cross = remote(pg.at[2], pgr.at[2], pg_s.at[2], pg_r.at[2], cross)

    up_cross = remote(upc_h, upr_o, uc_s.at[0], uc_r.at[0], cross)
    load_qkv.wait()

    def wait_block(b):
        for k in (1, 2, 3):

            @pl.when(flip(h, k) == b)
            def _():
                remote(gctx.at[0], gcr.at[b], gc_s.at[k], gc_r.at[k], at_head(k)).wait_recv()

    def attention(sequence):
        for i, t in enumerate(sequence[:2]):
            p_load(t, i).start()
        for i, t in enumerate(sequence):
            slot = i % 3
            if i + 2 < tiles:
                p_load(sequence[i + 2], (i + 2) % 3).start()
            b, sub = t // per_block, t % per_block
            if sub == 0:
                wait_block(b)
            p_load(t, slot).wait()
            size = min(t + 1, reach) * TILE
            first = (t + 1) * TILE - size
            grad = gcr[b, sub * TILE : (sub + 1) * TILE, :]
            meet = grad.astype(F32) * ctx[t].astype(F32)
            outs = []
            for a in range(heads):
                g = grad[:, a * hd : (a + 1) * hd]
                delta = jnp.sum(meet[:, a * hd : (a + 1) * hd], axis=1, keepdims=True)
                q = qkv[0, a, t * TILE : (t + 1) * TILE, :]
                k = qkv[1, a, first : (t + 1) * TILE, :]
                v = qkv[2, a, first : (t + 1) * TILE, :]
                p = p_v[slot, a, :, :size]
                ds = (p.astype(F32) * (dot(g, v, ((1,), (1,))) - delta)).astype(BF16)
                outs.append(dot(ds, k) * (hd ** (-0.5)))
                dk[a, first : (t + 1) * TILE, :] += dot(ds, q, ((0,), (0,)))
                dv[a, first : (t + 1) * TILE, :] += dot(p, g, ((0,), (0,)))
            grads[0, t * TILE : (t + 1) * TILE, :] = jnp.concatenate(outs, axis=1).astype(BF16)
            if i == 3:
                up_cross.start()

    half = tiles // 2

    @pl.when(h < 2)
    def _():
        attention(list(range(tiles)))

    @pl.when(h >= 2)
    def _():
        attention(list(range(half, tiles)) + list(range(half)))

    load_gath.start()
    for t in range(tiles):
        rows = slice(t * TILE, (t + 1) * TILE)
        grads[1, rows, :] = jnp.concatenate([dk[a, rows, :] for a in range(heads)], axis=1).astype(BF16)
        grads[2, rows, :] = jnp.concatenate([dv[a, rows, :] for a in range(heads)], axis=1).astype(BF16)

    def normed_block(index):
        at = pl.ds(pl.multiple_of(index * tok, tok), tok)
        total = dot(grads[0, at, :], w_ref[0])
        for c in (1, 2):
            total += dot(grads[c, at, :], w_ref[c])
        return total

    gn_sib = [remote(gsend.at[i], grecv.at[i], gn_s.at[i], gn_r.at[i], sib) for i in range(2)]
    gn_cross = remote(gacc, grecv.at[2], gn_s.at[2], gn_r.at[2], cross)
    gsend[1] = normed_block(flip(h, 3)).astype(BF16)
    gn_sib[1].start()
    mine = normed_block(flip(h, 2))
    gn_sib[1].wait_recv()
    gacc[...] = (mine + grecv[1].astype(F32)).astype(BF16)
    gn_cross.start()
    gsend[0] = normed_block(flip(h, 1)).astype(BF16)
    gn_sib[0].start()

    pg_sib[1].wait_recv()
    pg_sib[0].wait_recv()
    pg_sib[1].wait_send()
    for copy in sm_head:
        copy.wait_recv()
    smt[...] = sm_ref[...] + smr[1] + smr[2] + smr[3]
    sm_dp = [remote(smt, smd.at[r], sd_s.at[r], sd_r.at[r], at_dp(r)) for r in range(1, n_dp)]
    for copy in sm_dp:
        copy.start()
    pg[2] = (pg[2].astype(F32) + pgr[1].astype(F32)).astype(BF16)
    pg_cross.start()

    load_gath.wait()
    part = width // 3
    for c in range(3):
        for i in range(3):
            at = slice(i * part, (i + 1) * part)
            qg[c, at, :] = dot(gath[:, at], grads[c], ((0,), (0,))).astype(BF16)
    ones = jnp.ones((8, group), BF16)
    qb[...] = jnp.concatenate([dot(ones, grads[0]), dot(ones, grads[2])], axis=1)

    def send_qg(r):
        src = qg.at[:, pl.ds(pl.multiple_of(flip(d, r) * share, share), share), :]
        return remote(src, qgr.at[r], qg_s.at[r], qg_r.at[r], at_dp(r))

    def send_qb(r):
        return remote(qb, qbr.at[r], qb_s.at[r], qb_r.at[r], at_dp(r))

    for r in order:
        send_qg(r).start()
        send_qb(r).start()
    pg_cross.wait_recv()
    pg_sib[0].wait_send()
    pg[0] = (pacc[...] + pgr[0].astype(F32) + pgr[2].astype(F32)).astype(BF16)

    def send_pg(r):
        src = pg.at[0, pl.ds(pl.multiple_of(flip(d, r) * share, share), share), :]
        return remote(src, qgr.at[r, 3] if False else pgr.at[3, pl.ds(r * share, share), :], pt_s.at[r], pt_r.at[r], at_dp(r))

    for r in order:
        send_pg(r).start()
    own = normed_block(h)
    _, scaled, inverse = normalize(x_ref[...].astype(F32), g1_ref[...][None, :], b1_ref[...][None, :])
    gn_sib[0].wait_recv()
    own = own + grecv[0].astype(F32)
    gn_cross.wait_recv()
    own = own + grecv[2].astype(F32)
    en[0:1, :] = jnp.sum(own * scaled, axis=0, keepdims=True)
    en[1:2, :] = jnp.sum(own, axis=0, keepdims=True)
    en_head = [remote(en, enr.at[k], eh_s.at[k], eh_r.at[k], at_head(k)) for k in (1, 2, 3)]
    for copy in en_head:
        copy.start()
    igrad_o[...] = gres[...] + norm_backward(own, scaled, inverse, g1_ref[...][None, :])
    for copy in en_head:
        copy.wait_recv()
    ent[...] = en[...] + enr[1] + enr[2] + enr[3]
    en_dp = [remote(ent, enq.at[r], ed_s.at[r], ed_r.at[r], at_dp(r)) for r in range(1, n_dp)]
    for copy in en_dp:
        copy.start()

    for r in order:
        send_qg(r).wait_recv()
        send_qb(r).wait_recv()
        send_pg(r).wait_recv()
    here = pl.ds(pl.multiple_of(d * share, share), share)
    for c in range(3):
        total = qg[c, here, :].astype(F32)
        for r in range(1, n_dp):
            total += qgr[r, c].astype(F32)
        qg_o[c] = total
    total = pg[0, here, :].astype(F32)
    for r in range(1, n_dp):
        total += pgr[3, r * share : (r + 1) * share, :].astype(F32)
    pg_o[...] = total
    bias = qb[...]
    for r in range(1, n_dp):
        bias += qbr[r]
    qb_o[...] = bias
    for copy in sm_dp:
        copy.wait_recv()
    total = smt[...]
    for r in range(1, n_dp):
        total += smd[r]
    sums_o[...] = total
    for copy in bg_head:
        copy.wait_recv()
    bgs_o[...] = bg_ref[h] + bgr[1] + bgr[2] + bgr[3]
    for copy in en_dp:
        copy.wait_recv()
    total = ent[...]
    for r in range(1, n_dp):
        total += enq[r]
    ends_o[...] = total

    for k in (1, 2, 3):
        send_ctx(k).wait_send()
    for r in order:
        send_prod(r).wait()
        send_qg(r).wait_send()
        send_qb(r).wait_send()
        send_pg(r).wait_send()
    prod_own.wait()
    up_cross.wait()
    pg_cross.wait_send()
    gn_cross.wait_send()
    for copy in gn_sib + sm_head + bg_head + en_head + sm_dp + en_dp:
        copy.wait_send()


def stage_b(n_dp, gctx, qkv, probs, ctx, ctxf, gath, w, x, g1, b1, gres, prod, upc, sm, bg):
    tok, width = x.shape
    _, heads, group, hd = qkv.shape
    cols = heads * hd
    tiles = group // TILE
    span = probs.shape[3]
    share = width // n_dp
    sds = jax.ShapeDtypeStruct
    vm = pltpu.VMEM
    return pl.pallas_call(
        functools.partial(kernel_b, n_dp),
        out_shape=(
            sds((tok, width), F32),
            sds(prod.shape, BF16),
            sds(upc.shape, BF16),
            sds((3, share, cols), F32),
            sds((share, cols), F32),
            sds((8, 2 * cols), F32),
            sds(sm.shape, F32),
            sds((2, width), F32),
            sds(bg.shape[1:], F32),
        ),
        in_specs=[VM, ANY, ANY, VM, VM, ANY] + [VM] * 5 + [ANY, ANY, VM, VM],
        out_specs=(VM, ANY, ANY) + (VM,) * 6,
        scratch_shapes=[
            vm((4, tok, cols), BF16), vm((3, heads, group, hd), BF16), vm((3, heads, TILE, span), BF16), vm((group, width), BF16),
            vm((heads, group, hd), F32), vm((heads, group, hd), F32), vm((3, group, cols), BF16),
            vm((2, tok, width), BF16), vm((tok, width), BF16), vm((3, tok, width), BF16),
            vm((3, width, cols), BF16), vm((n_dp, 3, share, cols), BF16),
            vm((3, width, cols), BF16), vm((4, width, cols), BF16), vm((width, cols), F32),
            vm((8, 2 * cols), F32), vm((n_dp, 8, 2 * cols), F32),
            vm((4,) + sm.shape, F32), vm((n_dp,) + sm.shape, F32), vm(sm.shape, F32),
            vm((2, width), F32), vm((4, 2, width), F32), vm((2, width), F32), vm((n_dp, 2, width), F32),
            vm((4,) + bg.shape[1:], F32),
            DMA((2,)), DMA((3,)), DMA((4,)), DMA((4,)), DMA((n_dp,)), DMA((n_dp,)), DMA((1,)), DMA((1,)), DMA((3,)), DMA((3,)),
            DMA((n_dp,)), DMA((n_dp,)), DMA((3,)), DMA((3,)), DMA((n_dp,)), DMA((n_dp,)), DMA((n_dp,)), DMA((n_dp,)),
            DMA((4,)), DMA((4,)), DMA((n_dp,)), DMA((n_dp,)), DMA((4,)), DMA((4,)), DMA((n_dp,)), DMA((n_dp,)), DMA((4,)), DMA((4,)),
        ],
        compiler_params=pltpu.CompilerParams(collective_id=2, has_side_effects=True, vmem_limit_bytes=VMEM_LIMIT),
    )(gctx, qkv, probs, ctx, ctxf, gath, w.transpose(0, 2, 1), x, g1, b1, gres, prod, upc, sm, bg)


def local(
    block_input, norm1_gain, norm1_bias, qkv_weight, qkv_bias, proj_weight, proj_bias, norm2_gain, norm2_bias, router_weight,
    up_weight, up_bias, down_weight, down_bias, routes, lengths, cotangent,
):
    tok, width = block_input.shape
    experts = router_weight.shape[1]
    cap = 2 * tok // experts
    gath, qkv, probs, ctx, ctxf, projf, cots = stage_a(
        experts, block_input, norm1_gain, norm1_bias, qkv_weight, qkv_bias, proj_weight, routes, cotangent, lengths, cap
    )
    res, gate, prod, gres, gctx, upc, upo, dng, sm, bg, balance = stage_m(
        experts, block_input, ctxf, projf, proj_bias, norm2_gain, norm2_bias, router_weight, routes, cotangent, cots,
        up_weight, up_bias, down_weight, down_bias,
    )
    igrad, prodr, upr, qg, pg, qb, sums, ends, bgs = stage_b(
        experts, gctx, qkv, probs, ctx, ctxf, gath, qkv_weight, block_input, norm1_gain, norm1_bias, gres, prod, upc, sm, bg
    )
    d = lax.axis_index("dp")
    device = d * 4 + lax.axis_index("head")
    expert = routes[:, 0]
    hot = (expert[:, None] == jnp.arange(experts, dtype=jnp.int32)[None, :]).astype(jnp.int32)
    slot = jnp.sum(jnp.cumsum(hot, axis=0) * hot, axis=1) - 1
    mixed = (res + gate * prodr[(expert ^ d) * cap + slot].astype(F32)).astype(BF16)
    part = width // (4 * experts)

    def mine(row):
        return lax.dynamic_slice_in_dim(row, device * part, part, axis=0)

    hd = qkv_bias.shape[2]
    heads = qkv_bias.shape[1]
    qkv_bias_grad = lax.dynamic_slice_in_dim(qb[0].reshape(2, heads, hd), d * (hd // experts), hd // experts, axis=2)
    return (
        mixed, balance.reshape(1), igrad, mine(ends[0]), mine(ends[1]), qg, qkv_bias_grad, pg.T, mine(sums[2]), mine(sums[0]),
        mine(sums[1]), mine(sums[8 : 8 + experts].T), (upo + upr.astype(F32))[None], bgs[None, 0], dng[None], bgs[None, 1, : width // 4],
    )


def solution(mesh):
    placed = (
        P(("dp", "head"), None), P(), P(), P(None, None, "head"), P(None, "head", None), P("head", None), P(), P(), P(), P(),
        P("dp", None, None), P("dp", None), P("dp", None, None), P("dp", None), P(("dp", "head"), None), P("dp", None),
        P(("dp", "head"), None),
    )
    tokens = P(("dp", "head"))
    return jax.shard_map(
        local,
        mesh=mesh,
        in_specs=placed,
        out_specs=(
            P(("dp", "head"), None), tokens, P(("dp", "head"), None), tokens, tokens, P(None, "dp", "head"), P(None, "head", "dp"),
            P("head", "dp"), tokens, tokens, tokens, P(("dp", "head"), None), P("dp", None, "head"), P("dp", "head"),
            P("dp", "head", None), P("dp", "head"),
        ),
        check_vma=False,
    )
```

time: 880 us -> 291 us (0.33)
  waiting for transfers between devices: 273 us -> 0 us
  matrix products: 227 us -> 0 us
  Pallas kernels: 52.9 us -> 262 us
  other arithmetic: 129 us -> 7.82 us
  blocking collectives: 99.9 us -> 0 us
  local copies, waits for them, and re-layouts: 54.2 us -> 14.5 us
  between operations: 17.9 us -> 2.76 us
  starting transfers between devices: 11.7 us -> 0 us
    dot_general x34 -> x0, matrix products: 227 us -> none  [the longest x1 36 us: local(): jnp.dot(expert_rows, up_weight[0], preferred_element_type=jnp.float32)]
    pallas_call x0 -> x2, Pallas kernels: none -> 201 us  [the longest x1 116 us: stage_b(): pl.pallas_call(functools.partial(kernel_b, n_dp), out_shape=(sds((tok, wi...]
    reduce_scatter x3 -> x0, waiting for transfers between devices: 133 us -> none  [the longest x1 47.7 us: local(): lax.psum_scatter(up_grad[None].astype(jnp.bfloat16), 'head', scatter_dime...]
    all_to_all x3 -> x0, waiting for transfers between devices: 74.5 us -> none  [the longest x1 35.2 us: local(): lax.all_to_all(send_rows.reshape(num_experts, capacity, width), 'dp', spl...]
    sub x5 -> x1, other arithmetic: 69.6 us -> 0.01 us  [local(): slot = jnp.sum(jnp.cumsum(hot, axis=0) * hot, axis=1) - 1]
    unnamed x2 -> x0, blocking collectives: 61.4 us -> none
    unnamed x12 -> x0, waiting for transfers between devices: 53.9 us -> none
    all_to_all x1 -> x0, blocking collectives: 38.5 us -> none  [local(): lax.all_to_all(grad_rows.reshape(num_experts, capacity, width), 'dp', spl...]
  transfers between devices with their start and end apart: 11 -> 0, of which waited for: 8 -> 0; matrix products, arithmetic and copies ran while one was open for 34% -> 0% of each run, Pallas kernels for 0% -> 0%
where the time goes in v2:
time: 291 us; the launch traced here: 287 us
  Pallas kernels  262 us (90%)
  local copies, waits for them, and re-layouts  14.5 us (5%)
  other arithmetic  7.82 us (3%)
    pallas_call x1, Pallas kernels, stage_b(): pl.pallas_call(functools.partial(kernel_b, n_dp), out_shape=(sds((tok, wi...  116 us
    pallas_call x1, Pallas kernels, stage_m(): pl.pallas_call(functools.partial(kernel_m, n_dp), out_shape=(sds((tok, wi...  84.6 us
    pallas_call x1, Pallas kernels, stage_a(): pl.pallas_call(functools.partial(kernel_a, n_dp), out_shape=(sds((group,...  61.3 us

profile of v2, /device:TPU:0, one launch (start us, length us, event | category | flops | bytes accessed | tf_op | source)
XLA Modules:
  0.0 286.9 jit_solution(8053238261502883948)
XLA Ops:
  0.6 61.3 %shard_map.288 = (bf16[2048,768]{1,0:T(8,128)(2,1)}, bf16[3,3,2048,64]{3,2,1,0:T(8,128)(2,1)}, bf16[3,8,256,1280]{3,2,1,0:T(8,128)(2,1)}, bf16[8,256,192]{2,1,0:...) custom-call(bf16[512,768]{1,0:T(8,128)(2,1)} %x_ref.5, ...), custom_call_target="tpu_custom_call" | custom-call | tf_op jit(solution)/shard_map/pallas_call | solution.py:278
  62.0 84.6 %shard_map.289 = (f32[512,768]{1,0:T(8,128)}, f32[512,1]{1,0:T(8,128)}, bf16[1024,768]{1,0:T(8,128)(2,1)}, f32[512,768]{1,0:T(8,128)}, bf16[4,512,192]{2,1,0:T(8...) custom-call(bf16[512,768]{1,0:T(8,128)(2,1)} %x_ref.5, ...), custom_call_target="tpu_custom_call" | custom-call | tf_op jit(solution)/shard_map/pallas_call | solution.py:589
  146.6 115.9 %shard_map.290 = (f32[512,768]{1,0:T(8,128)}, bf16[1024,768]{1,0:T(8,128)(2,1)}, bf16[768,768]{1,0:T(8,128)(2,1)}, f32[3,96,192]{2,1,0:T(8,128)}, f32[96,192]{1,...) custom-call(bf16[4,512,192]{2,1,0:T(8,128)(2,1)} %get-tuple-element.48.gctx, ...), custom_call_target="tpu_custom_call" | custom-call | tf_op jit(solution)/shard_map/pallas_call | solution.py:903
  262.5 3.7 %add_bitcast_fusion = f32[1,768,768]{2,1,0:T(8,128)} fusion(f32[768,768]{1,0:T(8,128)} %get-tuple-element.66, bf16[768,768]{1,0:T(8,128)(2,1)} %get-tuple-element.67), kind=kLoop, calls=%fused_computation.1 | loop fusion | flops 1179648 | bytes 5898240 | tf_op jit(solution)/shard_map/broadcast_in_dim | solution.py:969
  266.3 0.6 fusion.4
  266.9 0.6 fusion.5
  267.5 0.6 fusion.6
  268.0 0.6 fusion.3
  268.6 0.6 fusion.2
  269.2 1.1 reduce-window.6
  270.4 0.2 slice_reduce_fusion
  270.8 2.0 gather_fusion
  272.8 0.1 reduce
  273.0 2.7 add_convert_fusion
  275.6 0.7 copy.36
  276.4 0.7 dynamic-slice_bitcast_fusion
  277.0 0.7 slice_reduce_fusion.1
  277.9 0.6 copy.35
  278.5 1.3 slice.42
  279.8 1.3 slice.43
  281.7 1.1 copy.42
  282.9 0.7 copy.43
  283.6 0.6 copy-done.1
  284.2 1.4 copy.44
  (28 shorter events, 0.4 us)
Async XLA Ops:
  262.5 3.8 %copy-start.7 = (f32[16,768]{1,0:T(8,128)S(1)}, f32[16,768]{1,0:T(8,128)}, u32[]{:S(2)}) copy-start(f32[16,768]{1,0:T(8,128)} %get-tuple-element.65) | copy-start | bytes 147460
  262.5 3.8 %copy-start.8 = (f32[2,768]{1,0:T(2,128)S(1)}, f32[2,768]{1,0:T(2,128)}, u32[]{:S(2)}) copy-start(f32[2,768]{1,0:T(2,128)} %get-tuple-element.61) | copy-start | bytes 18436
  262.5 6.7 %copy-start.6 = (s32[512,1]{0,1:T(1,128)S(1)}, s32[512,1]{0,1:T(1,128)}, u32[]{:S(2)}) copy-start(s32[512,1]{0,1:T(1,128)} %param.31) | copy-start | bytes 6148
  262.5 8.2 %copy-start = (bf16[1024,768]{1,0:T(8,128)(2,1)S(1)}, bf16[1024,768]{1,0:T(8,128)(2,1)}, u32[]{:S(2)}) copy-start(bf16[1024,768]{1,0:T(8,128)(2,1)} %get-tuple-element.58) | copy-start | bytes 4718596
  270.8 2.0 copy-start.4
  272.9 2.7 copy-start.5
  273.0 8.8 %copy-start.2 = (f32[512,768]{1,0:T(8,128)S(1)}, f32[512,768]{1,0:T(8,128)}, u32[]{:S(2)}) copy-start(f32[512,768]{1,0:T(8,128)} %get-tuple-element.127) | copy-start | bytes 4718596
  281.7 1.2 copy-start.3
  281.7 2.4 copy-start.1
